TPU v7x, 32 devices: a whole 2x2x4 slice. The times are simulated.
32 devices in a mesh: angle: 2 (over core), tile: 4 (over y, x), cuts: 4 (over z).
Axes of the slice: x: 2, y: 2, z: 4, core: 2. Of those that a mesh axis runs over, the one named last changes fastest.
Arguments:
- objects: float32 [2, 2, 512, 512], P('angle', None, ('tile', 'cuts')), may hold values from -6 to 6
- illumination: float32 [2, 128, 128], replicated, may hold values from -6 to 6
- positions: int32 [2, 256, 2], P('angle', ('tile', 'cuts')), may hold values from 0 to 384
- amplitudes: bfloat16 [2, 256, 128, 128], P('angle', ('tile', 'cuts')), may hold values from 0.25 to 2.5
- projector: bfloat16 [1024, 4096], P(None, ('angle', 'cuts')), may hold values from -0.1875 to 0.1875
Outputs:
- new_objects: float32 [2, 2, 512, 512], P('angle', None, ('tile', 'cuts'))
- volume: float32 [512, 4096], P('tile', ('angle', 'cuts'))
All inputs are finite; a program needn't handle non-finite values.
Results may differ from a plain program's by a relative error of at most 0.02.
Values may be sent and summed in bfloat16 or wider, within the bound.
No kernel may reach another device: no remote copies, remote signals or barrier semaphores. Data moves between devices by JAX's collectives and lax.ppermute only.
A program may use at most 64 MiB of HBM per device.

v0:
```python
import functools

import jax
import jax.numpy as jnp
import numpy as np
from jax import lax
from jax.experimental import pallas as pl
from jax.experimental.pallas import tpu as pltpu
from jax.sharding import PartitionSpec as P


step_size = 0.1
LANES = 128
GROUP = 16
VMEM_LIMIT = 24 * 2**20


def dft_table(width):
    index = np.arange(width)
    phase = (index[:, None] * index[None, :] % width) * (2.0 * np.pi / width)
    real = np.cos(phase) / np.sqrt(width)
    imag = -np.sin(phase) / np.sqrt(width)
    return jnp.asarray(np.stack([real, imag]).astype(jnp.bfloat16))


def dot(a, b):
    return jnp.dot(a, b, preferred_element_type=jnp.float32)


def patch_kernel(
    layout,
    place_ref,
    here_ref,
    *refs,
):
    (in_ids, out_ids, band_rows, _, cuts_count, group) = layout
    n_in, n_out = len(in_ids), len(out_ids)
    piece_refs = refs[:n_in]
    probe_ref, amp_ref, table_ref = refs[n_in : n_in + 3]
    out_refs = refs[n_in + 3 : n_in + 3 + n_out]
    image, canvas, exits, right_ref, left_ref = refs[n_in + 3 + n_out :]
    col_tiles = image.shape[1]
    edge = probe_ref.shape[-1]
    patches = amp_ref.shape[0]
    tile_at, cuts_at = here_ref[0], here_ref[1]

    def band_start(k, j):
        band = (tile_at ^ k) * cuts_count + (cuts_at ^ j)
        return pl.multiple_of(band * band_rows, band_rows)

    for ref, spots in zip(piece_refs, in_ids):
        for slot, (k, j) in enumerate(spots):
            rows = pl.ds(band_start(k, j), band_rows)
            for plane in range(2):
                for col in range(col_tiles):
                    image[plane, col, rows, :] = ref[
                        slot, plane, :, col * LANES : (col + 1) * LANES
                    ].astype(jnp.float32)
    canvas[...] = jnp.zeros_like(canvas)
    for top in range(2):
        for side in range(2):
            block = table_ref[top ^ side]
            here = (slice(top * edge, (top + 1) * edge), slice(side * edge, (side + 1) * edge))
            right_ref[here] = -block if top > side else block
            left_ref[here] = -block if top < side else block
    lane = lax.broadcasted_iota(jnp.int32, (edge, LANES), 1)

    def several(step, carry):
        spots = []
        for q in range(group):
            row_at = place_ref[group * step + q, 0]
            col_at = place_ref[group * step + q, 1]
            col = jnp.minimum(lax.div(col_at, LANES), col_tiles - 2)
            spots.append((pl.ds(row_at, edge), col, col_at - col * LANES))
        probe_real, probe_imag = probe_ref[0], probe_ref[1]
        stacked = []
        for q, (rows, col, shift) in enumerate(spots):
            back = (LANES - shift) & (LANES - 1)
            window = []
            for plane in range(2):
                near = image[plane, col, rows, :]
                far = image[plane, col + 1, rows, :]
                window.append(pltpu.roll(jnp.where(lane < shift, far, near), back, 1))
            exit_real = probe_real * window[0] - probe_imag * window[1]
            exit_imag = probe_real * window[1] + probe_imag * window[0]
            exits[q, 0] = exit_real
            exits[q, 1] = exit_imag
            stacked.append(jnp.concatenate([exit_real, exit_imag], 1).astype(jnp.bfloat16))
        spread = dot(jnp.concatenate(stacked, 0), right_ref[...]).astype(jnp.bfloat16)

        def side_by_side(x):
            halves = [
                jnp.concatenate(
                    [x[q * edge : (q + 1) * edge, h * edge : (h + 1) * edge] for q in range(group)], 1
                )
                for h in range(2)
            ]
            return jnp.concatenate(halves, 0)

        spectrum = dot(left_ref[...], side_by_side(spread))
        real, imag = spectrum[:edge], spectrum[edge:]
        amp = jnp.concatenate([amp_ref[group * step + q] for q in range(group)], 1)
        scale = amp.astype(jnp.float32) * lax.rsqrt(jnp.maximum(real * real + imag * imag, 1.0))
        real = (real * scale).astype(jnp.bfloat16)
        imag = (imag * scale).astype(jnp.bfloat16)
        projected = jnp.concatenate(
            [
                jnp.concatenate([part[:, q * edge : (q + 1) * edge] for part in (real, imag)], 1)
                for q in range(group)
            ],
            0,
        )
        back_half = dot(projected, left_ref[...]).astype(jnp.bfloat16)
        revised = dot(right_ref[...], side_by_side(back_half))
        for q, (rows, col, shift) in enumerate(spots):
            diff_real = revised[:edge, q * edge : (q + 1) * edge] - exits[q, 0]
            diff_imag = revised[edge:, q * edge : (q + 1) * edge] - exits[q, 1]
            terms = (
                step_size * (probe_real * diff_real + probe_imag * diff_imag),
                step_size * (probe_real * diff_imag - probe_imag * diff_real),
            )
            for plane in range(2):
                moved = pltpu.roll(terms[plane], shift & (LANES - 1), 1)
                near = canvas[plane, col, rows, :] + jnp.where(lane >= shift, moved, 0.0)
                far = canvas[plane, col + 1, rows, :] + jnp.where(lane < shift, moved, 0.0)
                canvas[plane, col, rows, :] = near
                canvas[plane, col + 1, rows, :] = far
        return carry

    lax.fori_loop(0, patches // group, several, 0)
    for ref, (plane, k) in zip(out_refs, out_ids):
        for j in range(cuts_count):
            rows = pl.ds(band_start(k, j), band_rows)
            for col in range(col_tiles):
                ref[j, :, col * LANES : (col + 1) * LANES] = canvas[plane, col, rows, :].astype(
                    jnp.bfloat16
                )


def volume_kernel(masks, cuts_count, at_ref, *refs):
    phase_refs = refs[: len(masks)]
    weight_ref, out_ref, rows_ref = refs[-3:]
    cuts_at, angle_at = at_ref[0], at_ref[1]
    band_rows, width = phase_refs[0].shape[1:]
    total = refs[len(masks)][...] if len(refs) > len(masks) + 3 else None
    for a, (mask, ref) in enumerate(zip(masks, phase_refs)):
        for j in range(cuts_count):
            rows = pl.ds(pl.multiple_of((cuts_at ^ j) * band_rows, band_rows), band_rows)
            rows_ref[a, rows, :] = ref[j]
        weight = weight_ref[pl.ds(pl.multiple_of((angle_at ^ mask) * width, width), width), :]
        part = dot(rows_ref[a], weight)
        total = part if total is None else total + part
    out_ref[...] = total


def swap(x, axis, mask):
    size = lax.axis_size(axis)
    return lax.ppermute(x, axis, [(i, i ^ mask) for i in range(size)])


def add_up(*terms):
    total = terms[0].astype(jnp.float32)
    for term in terms[1:]:
        total = total + term.astype(jnp.float32)
    return total


def compute(objects, illumination, positions, amplitudes, projector):
    cuts_count = lax.axis_size("cuts")
    tile_count = lax.axis_size("tile")
    angle_count = lax.axis_size("angle")
    band_rows, image_width = objects.shape[2:]
    edge = illumination.shape[-1]
    image_rows = band_rows * tile_count * cuts_count
    voxel_count = projector.shape[1]
    object_half = objects[0].astype(jnp.bfloat16)

    near = [object_half]
    for j in range(1, cuts_count):
        near.append(swap(object_half, "cuts", j))
    own_spread = []
    for k in range(1, tile_count):
        own_spread.append(swap(object_half, "tile", k))
    far = jnp.stack(near[1:])
    pieces = [(object_half[None], ((0, 0),)), (far, tuple((0, j) for j in range(1, cuts_count)))]
    pieces += [(own_spread[k - 1][None], ((k, 0),)) for k in range(1, tile_count)]
    for k in range(1, tile_count):
        pieces.append((swap(far, "tile", k), tuple((k, j) for j in range(1, cuts_count))))

    out_ids = tuple((plane, k) for plane in (1, 0) for k in range(tile_count))
    group = next(g for g in (GROUP, 8, 4, 2, 1) if amplitudes.shape[1] % g == 0)
    layout = (tuple(ids for _, ids in pieces), out_ids, band_rows, tile_count, cuts_count, group)
    tile_at, cuts_at, angle_at = (lax.axis_index(axis) for axis in ("tile", "cuts", "angle"))
    here = jnp.stack([tile_at, cuts_at]).astype(jnp.int32)
    vmem = pl.BlockSpec(memory_space=pltpu.VMEM)
    smem = pl.BlockSpec(memory_space=pltpu.SMEM)
    col_tiles = image_width // LANES
    outs = pl.pallas_call(
        functools.partial(patch_kernel, layout),
        out_shape=[
            jax.ShapeDtypeStruct((cuts_count, band_rows, image_width), jnp.bfloat16)
            for _ in out_ids
        ],
        in_specs=[smem, smem] + [vmem] * (len(pieces) + 3),
        out_specs=[vmem] * len(out_ids),
        scratch_shapes=[
            pltpu.VMEM((2, col_tiles, image_rows, LANES), jnp.float32),
            pltpu.VMEM((2, col_tiles, image_rows, LANES), jnp.float32),
            pltpu.VMEM((group, 2, edge, edge), jnp.float32),
            pltpu.VMEM((2 * edge, 2 * edge), jnp.bfloat16),
            pltpu.VMEM((2 * edge, 2 * edge), jnp.bfloat16),
        ],
        compiler_params=pltpu.CompilerParams(vmem_limit_bytes=VMEM_LIMIT),
    )(
        positions[0],
        here,
        *[piece for piece, _ in pieces],
        illumination,
        amplitudes[0],
        dft_table(edge),
    )
    imag_outs, real_outs = outs[:tile_count], outs[tile_count:]

    imag_part, real_part = (
        add_up(part[0], *[swap(part[k], "tile", k) for k in range(1, tile_count)]).astype(jnp.bfloat16)
        for part in (imag_outs, real_outs)
    )
    imag_sum = add_up(imag_part[0], *[swap(imag_part[j], "cuts", j) for j in range(1, cuts_count)])[None]
    own_real = add_up(real_part[0], *[swap(real_part[j], "cuts", j) for j in range(1, cuts_count)])
    share = jnp.stack([own_real, imag_sum[0]])
    new_objects = objects + share[None]
    phase = (object_half[1].astype(jnp.float32) + imag_sum).astype(jnp.bfloat16)
    own_phase = phase[0]
    rows = [own_phase]
    for j in range(1, cuts_count):
        rows.append(swap(own_phase, "cuts", j))
    phase = jnp.stack(rows)
    others = [swap(phase, "angle", a) for a in range(1, angle_count)]
    at = jnp.stack([cuts_at, angle_at]).astype(jnp.int32)
    volume_rows = cuts_count * band_rows

    def product(masks, blocks, *before):
        return pl.pallas_call(
            functools.partial(volume_kernel, masks, cuts_count),
            out_shape=jax.ShapeDtypeStruct((volume_rows, voxel_count), jnp.float32),
            in_specs=[smem] + [vmem] * (len(blocks) + len(before) + 1),
            out_specs=vmem,
            scratch_shapes=[pltpu.VMEM((len(masks), volume_rows, image_width), jnp.bfloat16)],
            compiler_params=pltpu.CompilerParams(vmem_limit_bytes=VMEM_LIMIT),
        )(at, *blocks, *before, projector)

    volume = product((0,), (phase,))
    if angle_count > 1:
        volume = product(tuple(range(1, angle_count)), others, volume)
    return new_objects, volume


def solution(mesh):
    in_specs = (
        P("angle", None, ("tile", "cuts"), None),
        P(),
        P("angle", ("tile", "cuts"), None),
        P("angle", ("tile", "cuts"), None, None),
        P(None, ("angle", "cuts")),
    )
    out_specs = (P("angle", None, ("tile", "cuts"), None), P("tile", ("angle", "cuts")))
    return jax.shard_map(compute, mesh=mesh, in_specs=in_specs, out_specs=out_specs, check_vma=False)
```

profile of v0, /device:TPU:0, one launch (start us, length us, event | category | flops | bytes accessed | tf_op | source)
XLA Modules:
  0.0 62.6 jit_solution(6376013439400641109)
XLA Ops:
  0.6 1.0 %convert_bitcast_fusion = bf16[2,32,512]{2,1,0:T(8,128)(2,1)S(1)} fusion(f32[1,2,32,512]{3,2,1,0:T(8,128)} %param.6), kind=kLoop, calls=%fused_computation.27 | loop fusion | flops 32768 | bytes 196608 | tf_op jit(solution)/shard_map/convert_element_type | solution.py:176
  1.6 5.1 %collective-permute-start.2 = (bf16[2,32,512]{2,1,0:T(8,128)(2,1)S(1)}, bf16[2,32,512]{2,1,0:T(8,128)(2,1)S(1)}, u32[]{:S(2)}, u32[]{:S(2)}) collective-permute-start(bf16[2,32,512]{2,1,0:T(8,128)(2,1)S(1)} %convert_bitcast_fusion), channel_id=1, source_target_pairs={{0,3},{1,2},{2,1},{3,0},{4,7},{5,6},{6,5},{7,4},{8,11},{9,10},{10,... | collective-permute-start | bytes 196616 | tf_op jit(solution)/shard_map/ppermute | solution.py:158
  7.4 1.8 %collective-permute-done.2 = bf16[2,32,512]{2,1,0:T(8,128)(2,1)S(1)} collective-permute-done((bf16[2,32,512]{2,1,0:T(8,128)(2,1)S(1)}, bf16[2,32,512]{2,1,0:T(8,128)(2,1)S(1)}, u32[]{:S(2)}, u32[]{:S(2)}) %collective-permute-start.2) | collective-permute-done | bytes 65568 | tf_op jit(solution)/shard_map/ppermute | solution.py:158
  9.2 3.1 %collective-permute-done.1 = bf16[2,32,512]{2,1,0:T(8,128)(2,1)S(1)} collective-permute-done((bf16[2,32,512]{2,1,0:T(8,128)(2,1)S(1)}, bf16[2,32,512]{2,1,0:T(8,128)(2,1)S(1)}, u32[]{:S(2)}, u32[]{:S(2)}) %collective-permute-start.1) | collective-permute-done | bytes 65568 | tf_op jit(solution)/shard_map/ppermute | solution.py:158
  12.4 2.5 %collective-permute-start.8 = (bf16[3,2,32,512]{3,2,1,0:T(8,128)(2,1)S(1)}, bf16[3,2,32,512]{3,2,1,0:T(8,128)(2,1)S(1)}, u32[]{:S(2)}, u32[]{:S(2)}) collective-permute-start(bf16[3,2,32,512]{3,2,1,0:T(8,128)(2,1)S(1)} %pad_maximum_fusion.refs_1_), channel_id=1, source_target_pairs={{0,12},{4,8},{8,4},{12,0},{1,13},{5,9},{9,5},{13,1},{2,14},{6,10},... | collective-permute-start | bytes 589832 | tf_op jit(solution)/shard_map/ppermute | solution.py:158
  16.0 2.4 %collective-permute-start.5 = (bf16[2,32,512]{2,1,0:T(8,128)(2,1)S(1)}, bf16[2,32,512]{2,1,0:T(8,128)(2,1)S(1)}, u32[]{:S(2)}, u32[]{:S(2)}) collective-permute-start(bf16[2,32,512]{2,1,0:T(8,128)(2,1)S(1)} %convert_bitcast_fusion), channel_id=1, source_target_pairs={{0,12},{4,8},{8,4},{12,0},{1,13},{5,9},{9,5},{13,1},{2,14},{6,10},... | collective-permute-start | bytes 196616 | tf_op jit(solution)/shard_map/ppermute | solution.py:158
  18.9 0.9 %convert_element_type.80.refs_0_ = bf16[1,2,32,512]{3,2,1,0:T(8,128)(2,1)S(1)} convert(f32[1,2,32,512]{3,2,1,0:T(8,128)} %param.6) | non-fusion elementwise | flops 32768 | bytes 196608 | tf_op jit(solution)/shard_map/convert_element_type | solution.py:176
  19.9 0.7 %copy-done.5 = s32[1,16,2]{1,2,0:T(2,128)S(1)} copy-done((s32[1,16,2]{1,2,0:T(2,128)S(1)}, s32[1,16,2]{1,2,0:T(2,128)}, u32[]{:S(2)}) %copy-start.5) | copy-done | bytes 152
  20.6 4.9 %collective-permute-done.5 = bf16[2,32,512]{2,1,0:T(8,128)(2,1)S(1)} collective-permute-done((bf16[2,32,512]{2,1,0:T(8,128)(2,1)S(1)}, bf16[2,32,512]{2,1,0:T(8,128)(2,1)S(1)}, u32[]{:S(2)}, u32[]{:S(2)}) %collective-permute-start.5) | collective-permute-done | bytes 65568 | tf_op jit(solution)/shard_map/ppermute | solution.py:158
  25.6 1.6 %collective-permute-start.3 = (bf16[2,32,512]{2,1,0:T(8,128)(2,1)S(1)}, bf16[2,32,512]{2,1,0:T(8,128)(2,1)S(1)}, u32[]{:S(2)}, u32[]{:S(2)}) collective-permute-start(bf16[2,32,512]{2,1,0:T(8,128)(2,1)S(1)} %convert_bitcast_fusion), channel_id=1, source_target_pairs={{0,4},{4,0},{8,12},{12,8},{1,5},{5,1},{9,13},{13,9},{2,6},{6,2},{1... | collective-permute-start | bytes 196616 | tf_op jit(solution)/shard_map/ppermute | solution.py:158
  27.3 2.5 %collective-permute-done.3 = bf16[2,32,512]{2,1,0:T(8,128)(2,1)S(1)} collective-permute-done((bf16[2,32,512]{2,1,0:T(8,128)(2,1)S(1)}, bf16[2,32,512]{2,1,0:T(8,128)(2,1)S(1)}, u32[]{:S(2)}, u32[]{:S(2)}) %collective-permute-start.3) | collective-permute-done | bytes 65568 | tf_op jit(solution)/shard_map/ppermute | solution.py:158
  29.9 3.5 %shard_map.77 = (bf16[4,32,512]{2,1,0:T(8,128)(2,1)S(1)}, bf16[4,32,512]{2,1,0:T(8,128)(2,1)S(1)}, bf16[4,32,512]{2,1,0:T(8,128)(2,1)S(1)}, bf16[4,32,512]{2,1,0...) custom-call(s32[16,2]{1,0:T(8,128)S(1)} %copy.8.place_ref, ...), custom_call_target="tpu_custom_call" | custom-call | tf_op jit(solution)/shard_map/pallas_call | solution.py:198
  33.3 1.7 %collective-permute-start.15 = (bf16[4,32,512]{2,1,0:T(8,128)(2,1)S(1)}, bf16[4,32,512]{2,1,0:T(8,128)(2,1)S(1)}, u32[]{:S(2)}, u32[]{:S(2)}) collective-permute-start(bf16[4,32,512]{2,1,0:T(8,128)(2,1)S(1)} %get-tuple-element.15), channel_id=1, source_target_pairs={{0,4},{4,0},{8,12},{12,8},{1,5},{5,1},{9,13},{13,9},{2,6},{6,2},{1... | collective-permute-start | bytes 393224 | tf_op jit(solution)/shard_map/ppermute | solution.py:158
  35.0 1.5 %collective-permute-start.16 = (bf16[4,32,512]{2,1,0:T(8,128)(2,1)S(1)}, bf16[4,32,512]{2,1,0:T(8,128)(2,1)S(1)}, u32[]{:S(2)}, u32[]{:S(2)}) collective-permute-start(bf16[4,32,512]{2,1,0:T(8,128)(2,1)S(1)} %get-tuple-element.16), channel_id=1, source_target_pairs={{0,8},{4,12},{8,0},{12,4},{1,9},{5,13},{9,1},{13,5},{2,10},{6,14},... | collective-permute-start | bytes 393224 | tf_op jit(solution)/shard_map/ppermute | solution.py:158
  37.0 1.6 %collective-permute-start.9 = (bf16[4,32,512]{2,1,0:T(8,128)(2,1)S(1)}, bf16[4,32,512]{2,1,0:T(8,128)(2,1)S(1)}, u32[]{:S(2)}, u32[]{:S(2)}) collective-permute-start(bf16[4,32,512]{2,1,0:T(8,128)(2,1)S(1)} %get-tuple-element.11), channel_id=1, source_target_pairs={{0,4},{4,0},{8,12},{12,8},{1,5},{5,1},{9,13},{13,9},{2,6},{6,2},{1... | collective-permute-start | bytes 393224 | tf_op jit(solution)/shard_map/ppermute | solution.py:158
  38.6 1.5 %collective-permute-start.10 = (bf16[4,32,512]{2,1,0:T(8,128)(2,1)S(1)}, bf16[4,32,512]{2,1,0:T(8,128)(2,1)S(1)}, u32[]{:S(2)}, u32[]{:S(2)}) collective-permute-start(bf16[4,32,512]{2,1,0:T(8,128)(2,1)S(1)} %get-tuple-element.12), channel_id=1, source_target_pairs={{0,8},{4,12},{8,0},{12,4},{1,9},{5,13},{9,1},{13,5},{2,10},{6,14},... | collective-permute-start | bytes 393224 | tf_op jit(solution)/shard_map/ppermute | solution.py:158
  40.1 2.2 %collective-permute-start.11 = (bf16[4,32,512]{2,1,0:T(8,128)(2,1)S(1)}, bf16[4,32,512]{2,1,0:T(8,128)(2,1)S(1)}, u32[]{:S(2)}, u32[]{:S(2)}) collective-permute-start(bf16[4,32,512]{2,1,0:T(8,128)(2,1)S(1)} %get-tuple-element.13), channel_id=1, source_target_pairs={{0,12},{4,8},{8,4},{12,0},{1,13},{5,9},{9,5},{13,1},{2,14},{6,10},... | collective-permute-start | bytes 393224 | tf_op jit(solution)/shard_map/ppermute | solution.py:158
  42.4 1.6 %collective-permute-done.17 = bf16[4,32,512]{2,1,0:T(8,128)(2,1)S(1)} collective-permute-done((bf16[4,32,512]{2,1,0:T(8,128)(2,1)S(1)}, bf16[4,32,512]{2,1,0:T(8,128)(2,1)S(1)}, u32[]{:S(2)}, u32[]{:S(2)}) %collective-permute-start.17) | collective-permute-done | bytes 131104 | tf_op jit(solution)/shard_map/ppermute | solution.py:158
  44.1 0.7 %collective-permute-start.20 = (bf16[32,512]{1,0:T(8,128)(2,1)S(1)}, bf16[32,512]{1,0:T(8,128)(2,1)S(1)}, u32[]{:S(2)}, u32[]{:S(2)}) collective-permute-start(bf16[32,512]{1,0:T(8,128)(2,1)S(1)} %get-tuple-element.24), channel_id=1, source_target_pairs={{0,3},{1,2},{2,1},{3,0},{4,7},{5,6},{6,5},{7,4},{8,11},{9,10},{10,... | collective-permute-start | bytes 98312 | tf_op jit(solution)/shard_map/ppermute | solution.py:158
  44.8 2.8 %collective-permute-start.19 = (bf16[32,512]{1,0:T(8,128)(2,1)S(1)}, bf16[32,512]{1,0:T(8,128)(2,1)S(1)}, u32[]{:S(2)}, u32[]{:S(2)}) collective-permute-start(bf16[32,512]{1,0:T(8,128)(2,1)S(1)} %get-tuple-element.25), channel_id=1, source_target_pairs={{0,2},{1,3},{2,0},{3,1},{4,6},{5,7},{6,4},{7,5},{8,10},{9,11},{10,... | collective-permute-start | bytes 98312 | tf_op jit(solution)/shard_map/ppermute | solution.py:158
  47.7 1.0 %collective-permute-start.12 = (bf16[32,512]{1,0:T(8,128)(2,1)S(1)}, bf16[32,512]{1,0:T(8,128)(2,1)S(1)}, u32[]{:S(2)}, u32[]{:S(2)}) collective-permute-start(bf16[32,512]{1,0:T(8,128)(2,1)S(1)} %get-tuple-element.20), channel_id=1, source_target_pairs={{0,1},{1,0},{2,3},{3,2},{4,5},{5,4},{6,7},{7,6},{8,9},{9,8},{10,11... | collective-permute-start | bytes 98312 | tf_op jit(solution)/shard_map/ppermute | solution.py:158
  48.7 0.7 %collective-permute-start.14 = (bf16[32,512]{1,0:T(8,128)(2,1)S(1)}, bf16[32,512]{1,0:T(8,128)(2,1)S(1)}, u32[]{:S(2)}, u32[]{:S(2)}) collective-permute-start(bf16[32,512]{1,0:T(8,128)(2,1)S(1)} %get-tuple-element.21), channel_id=1, source_target_pairs={{0,3},{1,2},{2,1},{3,0},{4,7},{5,6},{6,5},{7,4},{8,11},{9,10},{10,... | collective-permute-start | bytes 98312 | tf_op jit(solution)/shard_map/ppermute | solution.py:158
  49.4 1.9 %collective-permute-start.13 = (bf16[32,512]{1,0:T(8,128)(2,1)S(1)}, bf16[32,512]{1,0:T(8,128)(2,1)S(1)}, u32[]{:S(2)}, u32[]{:S(2)}) collective-permute-start(bf16[32,512]{1,0:T(8,128)(2,1)S(1)} %get-tuple-element.22), channel_id=1, source_target_pairs={{0,2},{1,3},{2,0},{3,1},{4,6},{5,7},{6,4},{7,5},{8,10},{9,11},{10,... | collective-permute-start | bytes 98312 | tf_op jit(solution)/shard_map/ppermute | solution.py:158
  51.3 2.3 %collective-permute-start.23 = (bf16[32,512]{1,0:T(8,128)(2,1)S(1)}, bf16[32,512]{1,0:T(8,128)(2,1)S(1)}, u32[]{:S(2)}, u32[]{:S(2)}) collective-permute-start(bf16[32,512]{1,0:T(8,128)(2,1)S(1)} %get-tuple-element.18), channel_id=1, source_target_pairs={{0,3},{1,2},{2,1},{3,0},{4,7},{5,6},{6,5},{7,4},{8,11},{9,10},{10,... | collective-permute-start | bytes 98312 | tf_op jit(solution)/shard_map/ppermute | solution.py:158
  53.6 1.1 %collective-permute-start.22 = (bf16[32,512]{1,0:T(8,128)(2,1)S(1)}, bf16[32,512]{1,0:T(8,128)(2,1)S(1)}, u32[]{:S(2)}, u32[]{:S(2)}) collective-permute-start(bf16[32,512]{1,0:T(8,128)(2,1)S(1)} %get-tuple-element.18), channel_id=1, source_target_pairs={{0,2},{1,3},{2,0},{3,1},{4,6},{5,7},{6,4},{7,5},{8,10},{9,11},{10,... | collective-permute-start | bytes 98312 | tf_op jit(solution)/shard_map/ppermute | solution.py:158
  54.7 1.0 %collective-permute-start.21 = (bf16[32,512]{1,0:T(8,128)(2,1)S(1)}, bf16[32,512]{1,0:T(8,128)(2,1)S(1)}, u32[]{:S(2)}, u32[]{:S(2)}) collective-permute-start(bf16[32,512]{1,0:T(8,128)(2,1)S(1)} %get-tuple-element.18), channel_id=1, source_target_pairs={{0,1},{1,0},{2,3},{3,2},{4,5},{5,4},{6,7},{7,6},{8,9},{9,8},{10,11... | collective-permute-start | bytes 98312 | tf_op jit(solution)/shard_map/ppermute | solution.py:158
  55.7 1.3 %collective-permute-done.23 = bf16[32,512]{1,0:T(8,128)(2,1)S(1)} collective-permute-done((bf16[32,512]{1,0:T(8,128)(2,1)S(1)}, bf16[32,512]{1,0:T(8,128)(2,1)S(1)}, u32[]{:S(2)}, u32[]{:S(2)}) %collective-permute-start.23) | collective-permute-done | bytes 32800 | tf_op jit(solution)/shard_map/ppermute | solution.py:158
  57.0 1.4 %collective-permute-done.22 = bf16[32,512]{1,0:T(8,128)(2,1)S(1)} collective-permute-done((bf16[32,512]{1,0:T(8,128)(2,1)S(1)}, bf16[32,512]{1,0:T(8,128)(2,1)S(1)}, u32[]{:S(2)}, u32[]{:S(2)}) %collective-permute-start.22) | collective-permute-done | bytes 32800 | tf_op jit(solution)/shard_map/ppermute | solution.py:158
  58.8 0.8 %copy-done.4 = f32[1,2,32,512]{3,2,1,0:T(8,128)S(1)} copy-done((f32[1,2,32,512]{3,2,1,0:T(8,128)S(1)}, f32[1,2,32,512]{3,2,1,0:T(8,128)}, u32[]{:S(2)}) %copy-start.4) | copy-done | bytes 131096
  59.6 0.7 %fusion = f32[1,2,32,512]{3,2,1,0:T(8,128)} fusion(f32[1,2,32,512]{3,2,1,0:T(8,128)S(1)} %copy-done.4, f32[1,32,512]{2,1,0:T(8,128)S(1)} %get-tuple-element.19, f32[1,32,512]{2,1,0:T(8,128)S(1)} %fusion.6), kind=kLoop, calls=%fused_computation.4 | loop fusion | flops 65536 | bytes 393216 | tf_op jit(solution)/shard_map/add | solution.py:231
  60.3 0.8 %shard_map.78.refs_1_ = f32[128,512]{1,0:T(8,128)S(1)} custom-call(s32[2]{0:T(128)S(1)} %pad_add_fusion.1.at_ref, bf16[4,32,512]{2,1,0:T(8,128)(2,1)S(1)} %pad_maximum_fusion.1.refs_0_, bf16[1024,512]{1,0:T(8,128)(2,1)S(1)} %copy-done), custom_call_target="tpu_custom_call" | custom-call | tf_op jit(solution)/shard_map/pallas_call | solution.py:243
  61.1 1.5 %shard_map.79 = f32[128,512]{1,0:T(8,128)} custom-call(s32[2]{0:T(128)S(1)} %pad_add_fusion.1.at_ref, bf16[4,32,512]{2,1,0:T(8,128)(2,1)S(1)} %collective-permute-done.24.refs_0_, f32[128,512]{1,0:T(8,128)S(1)} %shard_map.78.refs_1_, bf16[1024,512]{1,0:T(8,128)(2,1)S(1)} %copy-done), custom_call_target="tpu_custom_call" | custom-call | tf_op jit(solution)/shard_map/pallas_call | solution.py:243
  (47 shorter events, 3.6 us)
Async XLA Ops:
  0.6 29.2 %copy-start.1 = (bf16[1,16,128,128]{3,2,1,0:T(8,128)(2,1)S(1)}, bf16[1,16,128,128]{3,2,1,0:T(8,128)(2,1)}, u32[]{:S(2)}) copy-start(bf16[1,16,128,128]{3,2,1,0:T(8,128)(2,1)} %param.9) | copy-start | bytes 1572868
  1.6 7.6 %collective-permute-start.2 = (bf16[2,32,512]{2,1,0:T(8,128)(2,1)S(1)}, bf16[2,32,512]{2,1,0:T(8,128)(2,1)S(1)}, u32[]{:S(2)}, u32[]{:S(2)}) collective-permute-start(bf16[2,32,512]{2,1,0:T(8,128)(2,1)S(1)} %convert_bitcast_fusion), channel_id=1, source_target_pairs={{0,3},{1,2},{2,1},{3,0},{4,7},{5,6},{6,5},{7,4},{8,11},{9,10},{10,... | collective-permute-start | bytes 196616 | tf_op jit(solution)/shard_map/ppermute | solution.py:158
  6.8 5.6 %collective-permute-start.1 = (bf16[2,32,512]{2,1,0:T(8,128)(2,1)S(1)}, bf16[2,32,512]{2,1,0:T(8,128)(2,1)S(1)}, u32[]{:S(2)}, u32[]{:S(2)}) collective-permute-start(bf16[2,32,512]{2,1,0:T(8,128)(2,1)S(1)} %convert_bitcast_fusion), channel_id=1, source_target_pairs={{0,2},{1,3},{2,0},{3,1},{4,6},{5,7},{6,4},{7,5},{8,10},{9,11},{10,... | collective-permute-start | bytes 196616 | tf_op jit(solution)/shard_map/ppermute | solution.py:158
  6.8 5.6 %collective-permute-start = (bf16[2,32,512]{2,1,0:T(8,128)(2,1)S(1)}, bf16[2,32,512]{2,1,0:T(8,128)(2,1)S(1)}, u32[]{:S(2)}, u32[]{:S(2)}) collective-permute-start(bf16[2,32,512]{2,1,0:T(8,128)(2,1)S(1)} %convert_bitcast_fusion), channel_id=1, source_target_pairs={{0,1},{1,0},{2,3},{3,2},{4,5},{5,4},{6,7},{7,6},{8,9},{9,8},{10,11... | collective-permute-start | bytes 196616 | tf_op jit(solution)/shard_map/ppermute | solution.py:158
  12.4 17.5 %copy-start.2 = (f32[2,128,128]{2,1,0:T(8,128)S(1)}, f32[2,128,128]{2,1,0:T(8,128)}, u32[]{:S(2)}) copy-start(f32[2,128,128]{2,1,0:T(8,128)} %refs_8_.1) | copy-start | bytes 393220
  12.4 17.4 %collective-permute-start.8 = (bf16[3,2,32,512]{3,2,1,0:T(8,128)(2,1)S(1)}, bf16[3,2,32,512]{3,2,1,0:T(8,128)(2,1)S(1)}, u32[]{:S(2)}, u32[]{:S(2)}) collective-permute-start(bf16[3,2,32,512]{3,2,1,0:T(8,128)(2,1)S(1)} %pad_maximum_fusion.refs_1_), channel_id=1, source_target_pairs={{0,12},{4,8},{8,4},{12,0},{1,13},{5,9},{9,5},{13,1},{2,14},{6,10},... | collective-permute-start | bytes 589832 | tf_op jit(solution)/shard_map/ppermute | solution.py:158
  14.9 14.9 %collective-permute-start.7 = (bf16[3,2,32,512]{3,2,1,0:T(8,128)(2,1)S(1)}, bf16[3,2,32,512]{3,2,1,0:T(8,128)(2,1)S(1)}, u32[]{:S(2)}, u32[]{:S(2)}) collective-permute-start(bf16[3,2,32,512]{3,2,1,0:T(8,128)(2,1)S(1)} %pad_maximum_fusion.refs_1_), channel_id=1, source_target_pairs={{0,8},{4,12},{8,0},{12,4},{1,9},{5,13},{9,1},{13,5},{2,10},{6,14},... | collective-permute-start | bytes 589832 | tf_op jit(solution)/shard_map/ppermute | solution.py:158
  15.4 14.4 %collective-permute-start.6 = (bf16[3,2,32,512]{3,2,1,0:T(8,128)(2,1)S(1)}, bf16[3,2,32,512]{3,2,1,0:T(8,128)(2,1)S(1)}, u32[]{:S(2)}, u32[]{:S(2)}) collective-permute-start(bf16[3,2,32,512]{3,2,1,0:T(8,128)(2,1)S(1)} %pad_maximum_fusion.refs_1_), channel_id=1, source_target_pairs={{0,4},{4,0},{8,12},{12,8},{1,5},{5,1},{9,13},{13,9},{2,6},{6,2},{1... | collective-permute-start | bytes 589832 | tf_op jit(solution)/shard_map/ppermute | solution.py:158
  16.0 9.6 %collective-permute-start.5 = (bf16[2,32,512]{2,1,0:T(8,128)(2,1)S(1)}, bf16[2,32,512]{2,1,0:T(8,128)(2,1)S(1)}, u32[]{:S(2)}, u32[]{:S(2)}) collective-permute-start(bf16[2,32,512]{2,1,0:T(8,128)(2,1)S(1)} %convert_bitcast_fusion), channel_id=1, source_target_pairs={{0,12},{4,8},{8,4},{12,0},{1,13},{5,9},{9,5},{13,1},{2,14},{6,10},... | collective-permute-start | bytes 196616 | tf_op jit(solution)/shard_map/ppermute | solution.py:158
  18.4 8.9 %collective-permute-start.4 = (bf16[2,32,512]{2,1,0:T(8,128)(2,1)S(1)}, bf16[2,32,512]{2,1,0:T(8,128)(2,1)S(1)}, u32[]{:S(2)}, u32[]{:S(2)}) collective-permute-start(bf16[2,32,512]{2,1,0:T(8,128)(2,1)S(1)} %convert_bitcast_fusion), channel_id=1, source_target_pairs={{0,8},{4,12},{8,0},{12,4},{1,9},{5,13},{9,1},{13,5},{2,10},{6,14},... | collective-permute-start | bytes 196616 | tf_op jit(solution)/shard_map/ppermute | solution.py:158
  18.9 11.0 %copy-start.3 = (bf16[2,128,128]{2,1,0:T(8,128)(2,1)S(1)}, bf16[2,128,128]{2,1,0:T(8,128)(2,1)}, u32[]{:S(2)}) copy-start(bf16[2,128,128]{2,1,0:T(8,128)(2,1)} %constant.15.clone.refs_10_) | copy-start | bytes 196612
  19.9 0.7 %copy-start.5 = (s32[1,16,2]{1,2,0:T(2,128)S(1)}, s32[1,16,2]{1,2,0:T(2,128)}, u32[]{:S(2)}) copy-start(s32[1,16,2]{1,2,0:T(2,128)} %param.8) | copy-start | bytes 388
  25.6 4.3 %collective-permute-start.3 = (bf16[2,32,512]{2,1,0:T(8,128)(2,1)S(1)}, bf16[2,32,512]{2,1,0:T(8,128)(2,1)S(1)}, u32[]{:S(2)}, u32[]{:S(2)}) collective-permute-start(bf16[2,32,512]{2,1,0:T(8,128)(2,1)S(1)} %convert_bitcast_fusion), channel_id=1, source_target_pairs={{0,4},{4,0},{8,12},{12,8},{1,5},{5,1},{9,13},{13,9},{2,6},{6,2},{1... | collective-permute-start | bytes 196616 | tf_op jit(solution)/shard_map/ppermute | solution.py:158
  33.3 6.8 %collective-permute-start.15 = (bf16[4,32,512]{2,1,0:T(8,128)(2,1)S(1)}, bf16[4,32,512]{2,1,0:T(8,128)(2,1)S(1)}, u32[]{:S(2)}, u32[]{:S(2)}) collective-permute-start(bf16[4,32,512]{2,1,0:T(8,128)(2,1)S(1)} %get-tuple-element.15), channel_id=1, source_target_pairs={{0,4},{4,0},{8,12},{12,8},{1,5},{5,1},{9,13},{13,9},{2,6},{6,2},{1... | collective-permute-start | bytes 393224 | tf_op jit(solution)/shard_map/ppermute | solution.py:158
  35.0 7.3 %collective-permute-start.16 = (bf16[4,32,512]{2,1,0:T(8,128)(2,1)S(1)}, bf16[4,32,512]{2,1,0:T(8,128)(2,1)S(1)}, u32[]{:S(2)}, u32[]{:S(2)}) collective-permute-start(bf16[4,32,512]{2,1,0:T(8,128)(2,1)S(1)} %get-tuple-element.16), channel_id=1, source_target_pairs={{0,8},{4,12},{8,0},{12,4},{1,9},{5,13},{9,1},{13,5},{2,10},{6,14},... | collective-permute-start | bytes 393224 | tf_op jit(solution)/shard_map/ppermute | solution.py:158
  36.5 7.4 %collective-permute-start.17 = (bf16[4,32,512]{2,1,0:T(8,128)(2,1)S(1)}, bf16[4,32,512]{2,1,0:T(8,128)(2,1)S(1)}, u32[]{:S(2)}, u32[]{:S(2)}) collective-permute-start(bf16[4,32,512]{2,1,0:T(8,128)(2,1)S(1)} %get-tuple-element.17), channel_id=1, source_target_pairs={{0,12},{4,8},{8,4},{12,0},{1,13},{5,9},{9,5},{13,1},{2,14},{6,10},... | collective-permute-start | bytes 393224 | tf_op jit(solution)/shard_map/ppermute | solution.py:158
  37.0 7.8 %collective-permute-start.9 = (bf16[4,32,512]{2,1,0:T(8,128)(2,1)S(1)}, bf16[4,32,512]{2,1,0:T(8,128)(2,1)S(1)}, u32[]{:S(2)}, u32[]{:S(2)}) collective-permute-start(bf16[4,32,512]{2,1,0:T(8,128)(2,1)S(1)} %get-tuple-element.11), channel_id=1, source_target_pairs={{0,4},{4,0},{8,12},{12,8},{1,5},{5,1},{9,13},{13,9},{2,6},{6,2},{1... | collective-permute-start | bytes 393224 | tf_op jit(solution)/shard_map/ppermute | solution.py:158
  38.6 9.0 %collective-permute-start.10 = (bf16[4,32,512]{2,1,0:T(8,128)(2,1)S(1)}, bf16[4,32,512]{2,1,0:T(8,128)(2,1)S(1)}, u32[]{:S(2)}, u32[]{:S(2)}) collective-permute-start(bf16[4,32,512]{2,1,0:T(8,128)(2,1)S(1)} %get-tuple-element.12), channel_id=1, source_target_pairs={{0,8},{4,12},{8,0},{12,4},{1,9},{5,13},{9,1},{13,5},{2,10},{6,14},... | collective-permute-start | bytes 393224 | tf_op jit(solution)/shard_map/ppermute | solution.py:158
  40.1 7.5 %collective-permute-start.11 = (bf16[4,32,512]{2,1,0:T(8,128)(2,1)S(1)}, bf16[4,32,512]{2,1,0:T(8,128)(2,1)S(1)}, u32[]{:S(2)}, u32[]{:S(2)}) collective-permute-start(bf16[4,32,512]{2,1,0:T(8,128)(2,1)S(1)} %get-tuple-element.13), channel_id=1, source_target_pairs={{0,12},{4,8},{8,4},{12,0},{1,13},{5,9},{9,5},{13,1},{2,14},{6,10},... | collective-permute-start | bytes 393224 | tf_op jit(solution)/shard_map/ppermute | solution.py:158
  44.0 16.3 %copy-start = (bf16[1024,512]{1,0:T(8,128)(2,1)S(1)}, bf16[1024,512]{1,0:T(8,128)(2,1)}, u32[]{:S(2)}) copy-start(bf16[1024,512]{1,0:T(8,128)(2,1)} %refs_2_.1) | copy-start | bytes 3145732
  44.0 5.4 %collective-permute-start.18 = (bf16[32,512]{1,0:T(8,128)(2,1)S(1)}, bf16[32,512]{1,0:T(8,128)(2,1)S(1)}, u32[]{:S(2)}, u32[]{:S(2)}) collective-permute-start(bf16[32,512]{1,0:T(8,128)(2,1)S(1)} %get-tuple-element.23), channel_id=1, source_target_pairs={{0,1},{1,0},{2,3},{3,2},{4,5},{5,4},{6,7},{7,6},{8,9},{9,8},{10,11... | collective-permute-start | bytes 98312 | tf_op jit(solution)/shard_map/ppermute | solution.py:158
  44.1 7.1 %collective-permute-start.20 = (bf16[32,512]{1,0:T(8,128)(2,1)S(1)}, bf16[32,512]{1,0:T(8,128)(2,1)S(1)}, u32[]{:S(2)}, u32[]{:S(2)}) collective-permute-start(bf16[32,512]{1,0:T(8,128)(2,1)S(1)} %get-tuple-element.24), channel_id=1, source_target_pairs={{0,3},{1,2},{2,1},{3,0},{4,7},{5,6},{6,5},{7,4},{8,11},{9,10},{10,... | collective-permute-start | bytes 98312 | tf_op jit(solution)/shard_map/ppermute | solution.py:158
  44.8 6.4 %collective-permute-start.19 = (bf16[32,512]{1,0:T(8,128)(2,1)S(1)}, bf16[32,512]{1,0:T(8,128)(2,1)S(1)}, u32[]{:S(2)}, u32[]{:S(2)}) collective-permute-start(bf16[32,512]{1,0:T(8,128)(2,1)S(1)} %get-tuple-element.25), channel_id=1, source_target_pairs={{0,2},{1,3},{2,0},{3,1},{4,6},{5,7},{6,4},{7,5},{8,10},{9,11},{10,... | collective-permute-start | bytes 98312 | tf_op jit(solution)/shard_map/ppermute | solution.py:158
  47.7 7.0 %collective-permute-start.12 = (bf16[32,512]{1,0:T(8,128)(2,1)S(1)}, bf16[32,512]{1,0:T(8,128)(2,1)S(1)}, u32[]{:S(2)}, u32[]{:S(2)}) collective-permute-start(bf16[32,512]{1,0:T(8,128)(2,1)S(1)} %get-tuple-element.20), channel_id=1, source_target_pairs={{0,1},{1,0},{2,3},{3,2},{4,5},{5,4},{6,7},{7,6},{8,9},{9,8},{10,11... | collective-permute-start | bytes 98312 | tf_op jit(solution)/shard_map/ppermute | solution.py:158
  48.7 7.0 %collective-permute-start.14 = (bf16[32,512]{1,0:T(8,128)(2,1)S(1)}, bf16[32,512]{1,0:T(8,128)(2,1)S(1)}, u32[]{:S(2)}, u32[]{:S(2)}) collective-permute-start(bf16[32,512]{1,0:T(8,128)(2,1)S(1)} %get-tuple-element.21), channel_id=1, source_target_pairs={{0,3},{1,2},{2,1},{3,0},{4,7},{5,6},{6,5},{7,4},{8,11},{9,10},{10,... | collective-permute-start | bytes 98312 | tf_op jit(solution)/shard_map/ppermute | solution.py:158
  49.4 6.4 %collective-permute-start.13 = (bf16[32,512]{1,0:T(8,128)(2,1)S(1)}, bf16[32,512]{1,0:T(8,128)(2,1)S(1)}, u32[]{:S(2)}, u32[]{:S(2)}) collective-permute-start(bf16[32,512]{1,0:T(8,128)(2,1)S(1)} %get-tuple-element.22), channel_id=1, source_target_pairs={{0,2},{1,3},{2,0},{3,1},{4,6},{5,7},{6,4},{7,5},{8,10},{9,11},{10,... | collective-permute-start | bytes 98312 | tf_op jit(solution)/shard_map/ppermute | solution.py:158
  51.3 5.8 %collective-permute-start.23 = (bf16[32,512]{1,0:T(8,128)(2,1)S(1)}, bf16[32,512]{1,0:T(8,128)(2,1)S(1)}, u32[]{:S(2)}, u32[]{:S(2)}) collective-permute-start(bf16[32,512]{1,0:T(8,128)(2,1)S(1)} %get-tuple-element.18), channel_id=1, source_target_pairs={{0,3},{1,2},{2,1},{3,0},{4,7},{5,6},{6,5},{7,4},{8,11},{9,10},{10,... | collective-permute-start | bytes 98312 | tf_op jit(solution)/shard_map/ppermute | solution.py:158
  53.6 4.8 %collective-permute-start.22 = (bf16[32,512]{1,0:T(8,128)(2,1)S(1)}, bf16[32,512]{1,0:T(8,128)(2,1)S(1)}, u32[]{:S(2)}, u32[]{:S(2)}) collective-permute-start(bf16[32,512]{1,0:T(8,128)(2,1)S(1)} %get-tuple-element.18), channel_id=1, source_target_pairs={{0,2},{1,3},{2,0},{3,1},{4,6},{5,7},{6,4},{7,5},{8,10},{9,11},{10,... | collective-permute-start | bytes 98312 | tf_op jit(solution)/shard_map/ppermute | solution.py:158
  54.7 4.1 %collective-permute-start.21 = (bf16[32,512]{1,0:T(8,128)(2,1)S(1)}, bf16[32,512]{1,0:T(8,128)(2,1)S(1)}, u32[]{:S(2)}, u32[]{:S(2)}) collective-permute-start(bf16[32,512]{1,0:T(8,128)(2,1)S(1)} %get-tuple-element.18), channel_id=1, source_target_pairs={{0,1},{1,0},{2,3},{3,2},{4,5},{5,4},{6,7},{7,6},{8,9},{9,8},{10,11... | collective-permute-start | bytes 98312 | tf_op jit(solution)/shard_map/ppermute | solution.py:158
  58.7 0.9 %copy-start.4 = (f32[1,2,32,512]{3,2,1,0:T(8,128)S(1)}, f32[1,2,32,512]{3,2,1,0:T(8,128)}, u32[]{:S(2)}) copy-start(f32[1,2,32,512]{3,2,1,0:T(8,128)} %param.6) | copy-start | bytes 393220
  58.8 2.3 %collective-permute-start.24 = (bf16[4,32,512]{2,1,0:T(8,128)(2,1)S(1)}, bf16[4,32,512]{2,1,0:T(8,128)(2,1)S(1)}, u32[]{:S(2)}, u32[]{:S(2)}) collective-permute-start(bf16[4,32,512]{2,1,0:T(8,128)(2,1)S(1)} %pad_maximum_fusion.1.refs_0_), channel_id=1, source_target_pairs={{0,16},{16,0},{1,17},{17,1},{2,18},{18,2},{3,19},{19,3},{4,20},{20... | collective-permute-start | bytes 393224 | tf_op jit(solution)/shard_map/ppermute | solution.py:158
where the time goes:
time: 62.8 us; the launch traced here: 62.6 us
  starting transfers between devices  34.5 us (55%)
  waiting for transfers between devices  17 us (27%)
  Pallas kernels  5.72 us (9%)
  other arithmetic  2.97 us (5%)
  local copies, waits for them, and re-layouts  1.6 us (3%)
  between operations  0.81 us (1%)
    ppermute x25, starting transfers between devices, swap(): return lax.ppermute(x, axis, [(i, i ^ mask) for i in range(size)])  34.5 us
    ppermute x25, waiting for transfers between devices, swap(): return lax.ppermute(x, axis, [(i, i ^ mask) for i in range(size)])  17 us
    pallas_call x1, Pallas kernels, compute(): pl.pallas_call(functools.partial(patch_kernel, layout), out_shape=[jax.Sh...  3.46 us
    pallas_call x2, Pallas kernels, product(): pl.pallas_call(functools.partial(volume_kernel, masks, cuts_count), out_s...  2.26 us
    convert_element_type x2, other arithmetic, compute(): object_half = objects[0].astype(jnp.bfloat16)  1.92 us
    unnamed x12, local copies, waits for them, and re-layouts  1.5 us
  transfers between devices with their start and end apart: 25, of which 8 were waited for; matrix products, arithmetic and copies ran while one was open for 3% of the time, Pallas kernels for 1%

commit v1 on v0

--- a/solution.py
+++ b/solution.py
@@ -30,7 +30,6 @@
 def patch_kernel(
     layout,
     place_ref,
-    here_ref,
     *refs,
 ):
     (in_ids, out_ids, band_rows, _, cuts_count, group) = layout
@@ -38,11 +37,13 @@
     piece_refs = refs[:n_in]
     probe_ref, amp_ref, table_ref = refs[n_in : n_in + 3]
     out_refs = refs[n_in + 3 : n_in + 3 + n_out]
-    image, canvas, exits, right_ref, left_ref = refs[n_in + 3 + n_out :]
+    image, canvas, exits, right_ref, left_ref, places, place_sem = refs[n_in + 3 + n_out :]
+    fetch = pltpu.make_async_copy(place_ref, places, place_sem)
+    fetch.start()
     col_tiles = image.shape[1]
     edge = probe_ref.shape[-1]
     patches = amp_ref.shape[0]
-    tile_at, cuts_at = here_ref[0], here_ref[1]
+    tile_at, cuts_at = lax.axis_index("tile"), lax.axis_index("cuts")
 
     def band_start(k, j):
         band = (tile_at ^ k) * cuts_count + (cuts_at ^ j)
@@ -68,8 +69,8 @@
     def several(step, carry):
         spots = []
         for q in range(group):
-            row_at = place_ref[group * step + q, 0]
-            col_at = place_ref[group * step + q, 1]
+            row_at = places[group * step + q, 0]
+            col_at = places[group * step + q, 1]
             col = jnp.minimum(lax.div(col_at, LANES), col_tiles - 2)
             spots.append((pl.ds(row_at, edge), col, col_at - col * LANES))
         probe_real, probe_imag = probe_ref[0], probe_ref[1]
@@ -127,6 +128,7 @@
                 canvas[plane, col + 1, rows, :] = far
         return carry
 
+    fetch.wait()
     lax.fori_loop(0, patches // group, several, 0)
     for ref, (plane, k) in zip(out_refs, out_ids):
         for j in range(cuts_count):
@@ -137,10 +139,10 @@
                 )
 
 
-def volume_kernel(masks, cuts_count, at_ref, *refs):
+def volume_kernel(masks, cuts_count, *refs):
     phase_refs = refs[: len(masks)]
     weight_ref, out_ref, rows_ref = refs[-3:]
-    cuts_at, angle_at = at_ref[0], at_ref[1]
+    cuts_at, angle_at = lax.axis_index("cuts"), lax.axis_index("angle")
     band_rows, width = phase_refs[0].shape[1:]
     total = refs[len(masks)][...] if len(refs) > len(masks) + 3 else None
     for a, (mask, ref) in enumerate(zip(masks, phase_refs)):
@@ -190,8 +192,6 @@
     out_ids = tuple((plane, k) for plane in (1, 0) for k in range(tile_count))
     group = next(g for g in (GROUP, 8, 4, 2, 1) if amplitudes.shape[1] % g == 0)
     layout = (tuple(ids for _, ids in pieces), out_ids, band_rows, tile_count, cuts_count, group)
-    tile_at, cuts_at, angle_at = (lax.axis_index(axis) for axis in ("tile", "cuts", "angle"))
-    here = jnp.stack([tile_at, cuts_at]).astype(jnp.int32)
     vmem = pl.BlockSpec(memory_space=pltpu.VMEM)
     smem = pl.BlockSpec(memory_space=pltpu.SMEM)
     col_tiles = image_width // LANES
@@ -201,7 +201,7 @@
             jax.ShapeDtypeStruct((cuts_count, band_rows, image_width), jnp.bfloat16)
             for _ in out_ids
         ],
-        in_specs=[smem, smem] + [vmem] * (len(pieces) + 3),
+        in_specs=[pl.BlockSpec(memory_space=pl.ANY)] + [vmem] * (len(pieces) + 3),
         out_specs=[vmem] * len(out_ids),
         scratch_shapes=[
             pltpu.VMEM((2, col_tiles, image_rows, LANES), jnp.float32),
@@ -209,11 +209,12 @@
             pltpu.VMEM((group, 2, edge, edge), jnp.float32),
             pltpu.VMEM((2 * edge, 2 * edge), jnp.bfloat16),
             pltpu.VMEM((2 * edge, 2 * edge), jnp.bfloat16),
+            pltpu.SMEM(positions.shape[1:], jnp.int32),
+            pltpu.SemaphoreType.DMA,
         ],
         compiler_params=pltpu.CompilerParams(vmem_limit_bytes=VMEM_LIMIT),
     )(
         positions[0],
-        here,
         *[piece for piece, _ in pieces],
         illumination,
         amplitudes[0],
@@ -236,18 +237,17 @@
         rows.append(swap(own_phase, "cuts", j))
     phase = jnp.stack(rows)
     others = [swap(phase, "angle", a) for a in range(1, angle_count)]
-    at = jnp.stack([cuts_at, angle_at]).astype(jnp.int32)
     volume_rows = cuts_count * band_rows
 
     def product(masks, blocks, *before):
         return pl.pallas_call(
             functools.partial(volume_kernel, masks, cuts_count),
             out_shape=jax.ShapeDtypeStruct((volume_rows, voxel_count), jnp.float32),
-            in_specs=[smem] + [vmem] * (len(blocks) + len(before) + 1),
+            in_specs=[vmem] * (len(blocks) + len(before) + 1),
             out_specs=vmem,
             scratch_shapes=[pltpu.VMEM((len(masks), volume_rows, image_width), jnp.bfloat16)],
             compiler_params=pltpu.CompilerParams(vmem_limit_bytes=VMEM_LIMIT),
-        )(at, *blocks, *before, projector)
+        )(*blocks, *before, projector)
 
     volume = product((0,), (phase,))
     if angle_count > 1:

time: 62.8 us -> 61.4 us (0.978)
  Pallas kernels: 5.72 us -> 4.33 us
    pallas_call x2, Pallas kernels: 2.26 us -> 1.19 us  [product(): pl.pallas_call(functools.partial(volume_kernel, masks, cuts_count), out_s...]
  transfers between devices with their start and end apart: 25 -> 25, of which waited for: 8 -> 8; matrix products, arithmetic and copies ran while one was open for 3% -> 3% of each run, Pallas kernels for 1% -> 0%
where the time goes in v1:
time: 61.4 us; the launch traced here: 61.2 us
  starting transfers between devices  34.6 us (56%)
  waiting for transfers between devices  17.1 us (28%)
  Pallas kernels  4.33 us (7%)
  other arithmetic  2.79 us (5%)
  local copies, waits for them, and re-layouts  1.6 us (3%)
  between operations  0.81 us (1%)
    ppermute x25, starting transfers between devices, swap(): return lax.ppermute(x, axis, [(i, i ^ mask) for i in range(size)])  34.6 us
    ppermute x25, waiting for transfers between devices, swap(): return lax.ppermute(x, axis, [(i, i ^ mask) for i in range(size)])  17.1 us
    pallas_call x1, Pallas kernels, compute(): pl.pallas_call(functools.partial(patch_kernel, layout), out_shape=[jax.Sh...  3.14 us
    convert_element_type x2, other arithmetic, compute(): object_half = objects[0].astype(jnp.bfloat16)  1.89 us
    unnamed x12, local copies, waits for them, and re-layouts  1.5 us
  transfers between devices with their start and end apart: 25, of which 8 were waited for; matrix products, arithmetic and copies ran while one was open for 3% of the time, Pallas kernels for 0%

profile of v1, /device:TPU:0, one launch (start us, length us, event | category | flops | bytes accessed | tf_op | source)
XLA Modules:
  0.0 61.2 jit_solution(11656524068866338925)
XLA Ops:
  0.6 1.0 %convert_bitcast_fusion = bf16[2,32,512]{2,1,0:T(8,128)(2,1)S(1)} fusion(f32[1,2,32,512]{3,2,1,0:T(8,128)} %param.6), kind=kLoop, calls=%fused_computation.25 | loop fusion | flops 32768 | bytes 196608 | tf_op jit(solution)/shard_map/convert_element_type | solution.py:178
  1.6 5.1 %collective-permute-start.2 = (bf16[2,32,512]{2,1,0:T(8,128)(2,1)S(1)}, bf16[2,32,512]{2,1,0:T(8,128)(2,1)S(1)}, u32[]{:S(2)}, u32[]{:S(2)}) collective-permute-start(bf16[2,32,512]{2,1,0:T(8,128)(2,1)S(1)} %convert_bitcast_fusion), channel_id=1, source_target_pairs={{0,3},{1,2},{2,1},{3,0},{4,7},{5,6},{6,5},{7,4},{8,11},{9,10},{10,... | collective-permute-start | bytes 196616 | tf_op jit(solution)/shard_map/ppermute | solution.py:160
  6.8 0.6 %collective-permute-start = (bf16[2,32,512]{2,1,0:T(8,128)(2,1)S(1)}, bf16[2,32,512]{2,1,0:T(8,128)(2,1)S(1)}, u32[]{:S(2)}, u32[]{:S(2)}) collective-permute-start(bf16[2,32,512]{2,1,0:T(8,128)(2,1)S(1)} %convert_bitcast_fusion), channel_id=1, source_target_pairs={{0,1},{1,0},{2,3},{3,2},{4,5},{5,4},{6,7},{7,6},{8,9},{9,8},{10,11... | collective-permute-start | bytes 196616 | tf_op jit(solution)/shard_map/ppermute | solution.py:160
  7.4 1.8 %collective-permute-done.2 = bf16[2,32,512]{2,1,0:T(8,128)(2,1)S(1)} collective-permute-done((bf16[2,32,512]{2,1,0:T(8,128)(2,1)S(1)}, bf16[2,32,512]{2,1,0:T(8,128)(2,1)S(1)}, u32[]{:S(2)}, u32[]{:S(2)}) %collective-permute-start.2) | collective-permute-done | bytes 65568 | tf_op jit(solution)/shard_map/ppermute | solution.py:160
  9.2 3.1 %collective-permute-done.1 = bf16[2,32,512]{2,1,0:T(8,128)(2,1)S(1)} collective-permute-done((bf16[2,32,512]{2,1,0:T(8,128)(2,1)S(1)}, bf16[2,32,512]{2,1,0:T(8,128)(2,1)S(1)}, u32[]{:S(2)}, u32[]{:S(2)}) %collective-permute-start.1) | collective-permute-done | bytes 65568 | tf_op jit(solution)/shard_map/ppermute | solution.py:160
  12.4 2.5 %collective-permute-start.8 = (bf16[3,2,32,512]{3,2,1,0:T(8,128)(2,1)S(1)}, bf16[3,2,32,512]{3,2,1,0:T(8,128)(2,1)S(1)}, u32[]{:S(2)}, u32[]{:S(2)}) collective-permute-start(bf16[3,2,32,512]{3,2,1,0:T(8,128)(2,1)S(1)} %pad_maximum_fusion.refs_1_), channel_id=1, source_target_pairs={{0,12},{4,8},{8,4},{12,0},{1,13},{5,9},{9,5},{13,1},{2,14},{6,10},... | collective-permute-start | bytes 589832 | tf_op jit(solution)/shard_map/ppermute | solution.py:160
  16.0 2.4 %collective-permute-start.5 = (bf16[2,32,512]{2,1,0:T(8,128)(2,1)S(1)}, bf16[2,32,512]{2,1,0:T(8,128)(2,1)S(1)}, u32[]{:S(2)}, u32[]{:S(2)}) collective-permute-start(bf16[2,32,512]{2,1,0:T(8,128)(2,1)S(1)} %convert_bitcast_fusion), channel_id=1, source_target_pairs={{0,12},{4,8},{8,4},{12,0},{1,13},{5,9},{9,5},{13,1},{2,14},{6,10},... | collective-permute-start | bytes 196616 | tf_op jit(solution)/shard_map/ppermute | solution.py:160
  18.9 6.6 %collective-permute-done.5 = bf16[2,32,512]{2,1,0:T(8,128)(2,1)S(1)} collective-permute-done((bf16[2,32,512]{2,1,0:T(8,128)(2,1)S(1)}, bf16[2,32,512]{2,1,0:T(8,128)(2,1)S(1)}, u32[]{:S(2)}, u32[]{:S(2)}) %collective-permute-start.5) | collective-permute-done | bytes 65568 | tf_op jit(solution)/shard_map/ppermute | solution.py:160
  25.6 1.6 %collective-permute-start.3 = (bf16[2,32,512]{2,1,0:T(8,128)(2,1)S(1)}, bf16[2,32,512]{2,1,0:T(8,128)(2,1)S(1)}, u32[]{:S(2)}, u32[]{:S(2)}) collective-permute-start(bf16[2,32,512]{2,1,0:T(8,128)(2,1)S(1)} %convert_bitcast_fusion), channel_id=1, source_target_pairs={{0,4},{4,0},{8,12},{12,8},{1,5},{5,1},{9,13},{13,9},{2,6},{6,2},{1... | collective-permute-start | bytes 196616 | tf_op jit(solution)/shard_map/ppermute | solution.py:160
  27.2 0.9 %convert_element_type.80.refs_0_ = bf16[1,2,32,512]{3,2,1,0:T(8,128)(2,1)S(1)} convert(f32[1,2,32,512]{3,2,1,0:T(8,128)} %param.6) | non-fusion elementwise | flops 32768 | bytes 196608 | tf_op jit(solution)/shard_map/convert_element_type | solution.py:178
  28.2 0.7 %copy-done.5 = s32[1,16,2]{1,2,0:T(2,128)S(1)} copy-done((s32[1,16,2]{1,2,0:T(2,128)S(1)}, s32[1,16,2]{1,2,0:T(2,128)}, u32[]{:S(2)}) %copy-start.5) | copy-done | bytes 152
  28.9 0.9 %collective-permute-done.3 = bf16[2,32,512]{2,1,0:T(8,128)(2,1)S(1)} collective-permute-done((bf16[2,32,512]{2,1,0:T(8,128)(2,1)S(1)}, bf16[2,32,512]{2,1,0:T(8,128)(2,1)S(1)}, u32[]{:S(2)}, u32[]{:S(2)}) %collective-permute-start.3) | collective-permute-done | bytes 65568 | tf_op jit(solution)/shard_map/ppermute | solution.py:160
  29.9 3.1 %shard_map.77 = (bf16[4,32,512]{2,1,0:T(8,128)(2,1)S(1)}, bf16[4,32,512]{2,1,0:T(8,128)(2,1)S(1)}, bf16[4,32,512]{2,1,0:T(8,128)(2,1)S(1)}, bf16[4,32,512]{2,1,0...) custom-call(s32[16,2]{1,0:T(8,128)S(1)} %copy.8.place_ref, ...), custom_call_target="tpu_custom_call" | custom-call | tf_op jit(solution)/shard_map/pallas_call | solution.py:198
  33.0 1.7 %collective-permute-start.15 = (bf16[4,32,512]{2,1,0:T(8,128)(2,1)S(1)}, bf16[4,32,512]{2,1,0:T(8,128)(2,1)S(1)}, u32[]{:S(2)}, u32[]{:S(2)}) collective-permute-start(bf16[4,32,512]{2,1,0:T(8,128)(2,1)S(1)} %get-tuple-element.15), channel_id=1, source_target_pairs={{0,4},{4,0},{8,12},{12,8},{1,5},{5,1},{9,13},{13,9},{2,6},{6,2},{1... | collective-permute-start | bytes 393224 | tf_op jit(solution)/shard_map/ppermute | solution.py:160
  34.7 1.5 %collective-permute-start.16 = (bf16[4,32,512]{2,1,0:T(8,128)(2,1)S(1)}, bf16[4,32,512]{2,1,0:T(8,128)(2,1)S(1)}, u32[]{:S(2)}, u32[]{:S(2)}) collective-permute-start(bf16[4,32,512]{2,1,0:T(8,128)(2,1)S(1)} %get-tuple-element.16), channel_id=1, source_target_pairs={{0,8},{4,12},{8,0},{12,4},{1,9},{5,13},{9,1},{13,5},{2,10},{6,14},... | collective-permute-start | bytes 393224 | tf_op jit(solution)/shard_map/ppermute | solution.py:160
  36.6 1.6 %collective-permute-start.9 = (bf16[4,32,512]{2,1,0:T(8,128)(2,1)S(1)}, bf16[4,32,512]{2,1,0:T(8,128)(2,1)S(1)}, u32[]{:S(2)}, u32[]{:S(2)}) collective-permute-start(bf16[4,32,512]{2,1,0:T(8,128)(2,1)S(1)} %get-tuple-element.11), channel_id=1, source_target_pairs={{0,4},{4,0},{8,12},{12,8},{1,5},{5,1},{9,13},{13,9},{2,6},{6,2},{1... | collective-permute-start | bytes 393224 | tf_op jit(solution)/shard_map/ppermute | solution.py:160
  38.2 1.5 %collective-permute-start.10 = (bf16[4,32,512]{2,1,0:T(8,128)(2,1)S(1)}, bf16[4,32,512]{2,1,0:T(8,128)(2,1)S(1)}, u32[]{:S(2)}, u32[]{:S(2)}) collective-permute-start(bf16[4,32,512]{2,1,0:T(8,128)(2,1)S(1)} %get-tuple-element.12), channel_id=1, source_target_pairs={{0,8},{4,12},{8,0},{12,4},{1,9},{5,13},{9,1},{13,5},{2,10},{6,14},... | collective-permute-start | bytes 393224 | tf_op jit(solution)/shard_map/ppermute | solution.py:160
  39.7 2.3 %collective-permute-start.11 = (bf16[4,32,512]{2,1,0:T(8,128)(2,1)S(1)}, bf16[4,32,512]{2,1,0:T(8,128)(2,1)S(1)}, u32[]{:S(2)}, u32[]{:S(2)}) collective-permute-start(bf16[4,32,512]{2,1,0:T(8,128)(2,1)S(1)} %get-tuple-element.13), channel_id=1, source_target_pairs={{0,12},{4,8},{8,4},{12,0},{1,13},{5,9},{9,5},{13,1},{2,14},{6,10},... | collective-permute-start | bytes 393224 | tf_op jit(solution)/shard_map/ppermute | solution.py:160
  42.0 1.6 %collective-permute-done.17 = bf16[4,32,512]{2,1,0:T(8,128)(2,1)S(1)} collective-permute-done((bf16[4,32,512]{2,1,0:T(8,128)(2,1)S(1)}, bf16[4,32,512]{2,1,0:T(8,128)(2,1)S(1)}, u32[]{:S(2)}, u32[]{:S(2)}) %collective-permute-start.17) | collective-permute-done | bytes 131104 | tf_op jit(solution)/shard_map/ppermute | solution.py:160
  43.8 0.7 %collective-permute-start.20 = (bf16[32,512]{1,0:T(8,128)(2,1)S(1)}, bf16[32,512]{1,0:T(8,128)(2,1)S(1)}, u32[]{:S(2)}, u32[]{:S(2)}) collective-permute-start(bf16[32,512]{1,0:T(8,128)(2,1)S(1)} %get-tuple-element.24), channel_id=1, source_target_pairs={{0,3},{1,2},{2,1},{3,0},{4,7},{5,6},{6,5},{7,4},{8,11},{9,10},{10,... | collective-permute-start | bytes 98312 | tf_op jit(solution)/shard_map/ppermute | solution.py:160
  44.5 2.7 %collective-permute-start.19 = (bf16[32,512]{1,0:T(8,128)(2,1)S(1)}, bf16[32,512]{1,0:T(8,128)(2,1)S(1)}, u32[]{:S(2)}, u32[]{:S(2)}) collective-permute-start(bf16[32,512]{1,0:T(8,128)(2,1)S(1)} %get-tuple-element.25), channel_id=1, source_target_pairs={{0,2},{1,3},{2,0},{3,1},{4,6},{5,7},{6,4},{7,5},{8,10},{9,11},{10,... | collective-permute-start | bytes 98312 | tf_op jit(solution)/shard_map/ppermute | solution.py:160
  47.4 1.0 %collective-permute-start.12 = (bf16[32,512]{1,0:T(8,128)(2,1)S(1)}, bf16[32,512]{1,0:T(8,128)(2,1)S(1)}, u32[]{:S(2)}, u32[]{:S(2)}) collective-permute-start(bf16[32,512]{1,0:T(8,128)(2,1)S(1)} %get-tuple-element.20), channel_id=1, source_target_pairs={{0,1},{1,0},{2,3},{3,2},{4,5},{5,4},{6,7},{7,6},{8,9},{9,8},{10,11... | collective-permute-start | bytes 98312 | tf_op jit(solution)/shard_map/ppermute | solution.py:160
  48.4 0.7 %collective-permute-start.14 = (bf16[32,512]{1,0:T(8,128)(2,1)S(1)}, bf16[32,512]{1,0:T(8,128)(2,1)S(1)}, u32[]{:S(2)}, u32[]{:S(2)}) collective-permute-start(bf16[32,512]{1,0:T(8,128)(2,1)S(1)} %get-tuple-element.21), channel_id=1, source_target_pairs={{0,3},{1,2},{2,1},{3,0},{4,7},{5,6},{6,5},{7,4},{8,11},{9,10},{10,... | collective-permute-start | bytes 98312 | tf_op jit(solution)/shard_map/ppermute | solution.py:160
  49.1 1.8 %collective-permute-start.13 = (bf16[32,512]{1,0:T(8,128)(2,1)S(1)}, bf16[32,512]{1,0:T(8,128)(2,1)S(1)}, u32[]{:S(2)}, u32[]{:S(2)}) collective-permute-start(bf16[32,512]{1,0:T(8,128)(2,1)S(1)} %get-tuple-element.22), channel_id=1, source_target_pairs={{0,2},{1,3},{2,0},{3,1},{4,6},{5,7},{6,4},{7,5},{8,10},{9,11},{10,... | collective-permute-start | bytes 98312 | tf_op jit(solution)/shard_map/ppermute | solution.py:160
  51.0 2.3 %collective-permute-start.23 = (bf16[32,512]{1,0:T(8,128)(2,1)S(1)}, bf16[32,512]{1,0:T(8,128)(2,1)S(1)}, u32[]{:S(2)}, u32[]{:S(2)}) collective-permute-start(bf16[32,512]{1,0:T(8,128)(2,1)S(1)} %get-tuple-element.18), channel_id=1, source_target_pairs={{0,3},{1,2},{2,1},{3,0},{4,7},{5,6},{6,5},{7,4},{8,11},{9,10},{10,... | collective-permute-start | bytes 98312 | tf_op jit(solution)/shard_map/ppermute | solution.py:160
  53.3 1.1 %collective-permute-start.22 = (bf16[32,512]{1,0:T(8,128)(2,1)S(1)}, bf16[32,512]{1,0:T(8,128)(2,1)S(1)}, u32[]{:S(2)}, u32[]{:S(2)}) collective-permute-start(bf16[32,512]{1,0:T(8,128)(2,1)S(1)} %get-tuple-element.18), channel_id=1, source_target_pairs={{0,2},{1,3},{2,0},{3,1},{4,6},{5,7},{6,4},{7,5},{8,10},{9,11},{10,... | collective-permute-start | bytes 98312 | tf_op jit(solution)/shard_map/ppermute | solution.py:160
  54.4 1.0 %collective-permute-start.21 = (bf16[32,512]{1,0:T(8,128)(2,1)S(1)}, bf16[32,512]{1,0:T(8,128)(2,1)S(1)}, u32[]{:S(2)}, u32[]{:S(2)}) collective-permute-start(bf16[32,512]{1,0:T(8,128)(2,1)S(1)} %get-tuple-element.18), channel_id=1, source_target_pairs={{0,1},{1,0},{2,3},{3,2},{4,5},{5,4},{6,7},{7,6},{8,9},{9,8},{10,11... | collective-permute-start | bytes 98312 | tf_op jit(solution)/shard_map/ppermute | solution.py:160
  55.4 1.3 %collective-permute-done.23 = bf16[32,512]{1,0:T(8,128)(2,1)S(1)} collective-permute-done((bf16[32,512]{1,0:T(8,128)(2,1)S(1)}, bf16[32,512]{1,0:T(8,128)(2,1)S(1)}, u32[]{:S(2)}, u32[]{:S(2)}) %collective-permute-start.23) | collective-permute-done | bytes 32800 | tf_op jit(solution)/shard_map/ppermute | solution.py:160
  56.7 1.4 %collective-permute-done.22 = bf16[32,512]{1,0:T(8,128)(2,1)S(1)} collective-permute-done((bf16[32,512]{1,0:T(8,128)(2,1)S(1)}, bf16[32,512]{1,0:T(8,128)(2,1)S(1)}, u32[]{:S(2)}, u32[]{:S(2)}) %collective-permute-start.22) | collective-permute-done | bytes 32800 | tf_op jit(solution)/shard_map/ppermute | solution.py:160
  58.6 0.8 %copy-done.4 = f32[1,2,32,512]{3,2,1,0:T(8,128)S(1)} copy-done((f32[1,2,32,512]{3,2,1,0:T(8,128)S(1)}, f32[1,2,32,512]{3,2,1,0:T(8,128)}, u32[]{:S(2)}) %copy-start.4) | copy-done | bytes 131096
  59.4 0.7 %fusion = f32[1,2,32,512]{3,2,1,0:T(8,128)} fusion(f32[1,2,32,512]{3,2,1,0:T(8,128)S(1)} %copy-done.4, f32[1,32,512]{2,1,0:T(8,128)S(1)} %get-tuple-element.19, f32[1,32,512]{2,1,0:T(8,128)S(1)} %fusion.6), kind=kLoop, calls=%fused_computation.4 | loop fusion | flops 65536 | bytes 393216 | tf_op jit(solution)/shard_map/add | solution.py:232
  60.3 1.0 %shard_map.79 = f32[128,512]{1,0:T(8,128)} custom-call(bf16[4,32,512]{2,1,0:T(8,128)(2,1)S(1)} %collective-permute-done.24.refs_0_, f32[128,512]{1,0:T(8,128)S(1)} %shard_map.78.refs_1_, bf16[1024,512]{1,0:T(8,128)(2,1)S(1)} %copy-done), custom_call_target="tpu_custom_call" | custom-call | tf_op jit(solution)/shard_map/pallas_call | solution.py:243
  (45 shorter events, 3.0 us)
Async XLA Ops:
  0.6 29.2 %copy-start.1 = (bf16[1,16,128,128]{3,2,1,0:T(8,128)(2,1)S(1)}, bf16[1,16,128,128]{3,2,1,0:T(8,128)(2,1)}, u32[]{:S(2)}) copy-start(bf16[1,16,128,128]{3,2,1,0:T(8,128)(2,1)} %param.9) | copy-start | bytes 1572868
  1.6 7.6 %collective-permute-start.2 = (bf16[2,32,512]{2,1,0:T(8,128)(2,1)S(1)}, bf16[2,32,512]{2,1,0:T(8,128)(2,1)S(1)}, u32[]{:S(2)}, u32[]{:S(2)}) collective-permute-start(bf16[2,32,512]{2,1,0:T(8,128)(2,1)S(1)} %convert_bitcast_fusion), channel_id=1, source_target_pairs={{0,3},{1,2},{2,1},{3,0},{4,7},{5,6},{6,5},{7,4},{8,11},{9,10},{10,... | collective-permute-start | bytes 196616 | tf_op jit(solution)/shard_map/ppermute | solution.py:160
  6.8 5.6 %collective-permute-start.1 = (bf16[2,32,512]{2,1,0:T(8,128)(2,1)S(1)}, bf16[2,32,512]{2,1,0:T(8,128)(2,1)S(1)}, u32[]{:S(2)}, u32[]{:S(2)}) collective-permute-start(bf16[2,32,512]{2,1,0:T(8,128)(2,1)S(1)} %convert_bitcast_fusion), channel_id=1, source_target_pairs={{0,2},{1,3},{2,0},{3,1},{4,6},{5,7},{6,4},{7,5},{8,10},{9,11},{10,... | collective-permute-start | bytes 196616 | tf_op jit(solution)/shard_map/ppermute | solution.py:160
  6.8 5.6 %collective-permute-start = (bf16[2,32,512]{2,1,0:T(8,128)(2,1)S(1)}, bf16[2,32,512]{2,1,0:T(8,128)(2,1)S(1)}, u32[]{:S(2)}, u32[]{:S(2)}) collective-permute-start(bf16[2,32,512]{2,1,0:T(8,128)(2,1)S(1)} %convert_bitcast_fusion), channel_id=1, source_target_pairs={{0,1},{1,0},{2,3},{3,2},{4,5},{5,4},{6,7},{7,6},{8,9},{9,8},{10,11... | collective-permute-start | bytes 196616 | tf_op jit(solution)/shard_map/ppermute | solution.py:160
  12.4 17.5 %copy-start.2 = (f32[2,128,128]{2,1,0:T(8,128)S(1)}, f32[2,128,128]{2,1,0:T(8,128)}, u32[]{:S(2)}) copy-start(f32[2,128,128]{2,1,0:T(8,128)} %refs_8_.1) | copy-start | bytes 393220
  12.4 17.5 %copy-start.3 = (bf16[2,128,128]{2,1,0:T(8,128)(2,1)S(1)}, bf16[2,128,128]{2,1,0:T(8,128)(2,1)}, u32[]{:S(2)}) copy-start(bf16[2,128,128]{2,1,0:T(8,128)(2,1)} %constant.2.clone.refs_10_) | copy-start | bytes 196612
  12.4 17.4 %collective-permute-start.8 = (bf16[3,2,32,512]{3,2,1,0:T(8,128)(2,1)S(1)}, bf16[3,2,32,512]{3,2,1,0:T(8,128)(2,1)S(1)}, u32[]{:S(2)}, u32[]{:S(2)}) collective-permute-start(bf16[3,2,32,512]{3,2,1,0:T(8,128)(2,1)S(1)} %pad_maximum_fusion.refs_1_), channel_id=1, source_target_pairs={{0,12},{4,8},{8,4},{12,0},{1,13},{5,9},{9,5},{13,1},{2,14},{6,10},... | collective-permute-start | bytes 589832 | tf_op jit(solution)/shard_map/ppermute | solution.py:160
  14.9 14.9 %collective-permute-start.7 = (bf16[3,2,32,512]{3,2,1,0:T(8,128)(2,1)S(1)}, bf16[3,2,32,512]{3,2,1,0:T(8,128)(2,1)S(1)}, u32[]{:S(2)}, u32[]{:S(2)}) collective-permute-start(bf16[3,2,32,512]{3,2,1,0:T(8,128)(2,1)S(1)} %pad_maximum_fusion.refs_1_), channel_id=1, source_target_pairs={{0,8},{4,12},{8,0},{12,4},{1,9},{5,13},{9,1},{13,5},{2,10},{6,14},... | collective-permute-start | bytes 589832 | tf_op jit(solution)/shard_map/ppermute | solution.py:160
  15.4 14.4 %collective-permute-start.6 = (bf16[3,2,32,512]{3,2,1,0:T(8,128)(2,1)S(1)}, bf16[3,2,32,512]{3,2,1,0:T(8,128)(2,1)S(1)}, u32[]{:S(2)}, u32[]{:S(2)}) collective-permute-start(bf16[3,2,32,512]{3,2,1,0:T(8,128)(2,1)S(1)} %pad_maximum_fusion.refs_1_), channel_id=1, source_target_pairs={{0,4},{4,0},{8,12},{12,8},{1,5},{5,1},{9,13},{13,9},{2,6},{6,2},{1... | collective-permute-start | bytes 589832 | tf_op jit(solution)/shard_map/ppermute | solution.py:160
  16.0 9.6 %collective-permute-start.5 = (bf16[2,32,512]{2,1,0:T(8,128)(2,1)S(1)}, bf16[2,32,512]{2,1,0:T(8,128)(2,1)S(1)}, u32[]{:S(2)}, u32[]{:S(2)}) collective-permute-start(bf16[2,32,512]{2,1,0:T(8,128)(2,1)S(1)} %convert_bitcast_fusion), channel_id=1, source_target_pairs={{0,12},{4,8},{8,4},{12,0},{1,13},{5,9},{9,5},{13,1},{2,14},{6,10},... | collective-permute-start | bytes 196616 | tf_op jit(solution)/shard_map/ppermute | solution.py:160
  18.4 10.5 %collective-permute-start.4 = (bf16[2,32,512]{2,1,0:T(8,128)(2,1)S(1)}, bf16[2,32,512]{2,1,0:T(8,128)(2,1)S(1)}, u32[]{:S(2)}, u32[]{:S(2)}) collective-permute-start(bf16[2,32,512]{2,1,0:T(8,128)(2,1)S(1)} %convert_bitcast_fusion), channel_id=1, source_target_pairs={{0,8},{4,12},{8,0},{12,4},{1,9},{5,13},{9,1},{13,5},{2,10},{6,14},... | collective-permute-start | bytes 196616 | tf_op jit(solution)/shard_map/ppermute | solution.py:160
  25.6 4.3 %collective-permute-start.3 = (bf16[2,32,512]{2,1,0:T(8,128)(2,1)S(1)}, bf16[2,32,512]{2,1,0:T(8,128)(2,1)S(1)}, u32[]{:S(2)}, u32[]{:S(2)}) collective-permute-start(bf16[2,32,512]{2,1,0:T(8,128)(2,1)S(1)} %convert_bitcast_fusion), channel_id=1, source_target_pairs={{0,4},{4,0},{8,12},{12,8},{1,5},{5,1},{9,13},{13,9},{2,6},{6,2},{1... | collective-permute-start | bytes 196616 | tf_op jit(solution)/shard_map/ppermute | solution.py:160
  28.1 0.7 %copy-start.5 = (s32[1,16,2]{1,2,0:T(2,128)S(1)}, s32[1,16,2]{1,2,0:T(2,128)}, u32[]{:S(2)}) copy-start(s32[1,16,2]{1,2,0:T(2,128)} %param.8) | copy-start | bytes 388
  33.0 6.7 %collective-permute-start.15 = (bf16[4,32,512]{2,1,0:T(8,128)(2,1)S(1)}, bf16[4,32,512]{2,1,0:T(8,128)(2,1)S(1)}, u32[]{:S(2)}, u32[]{:S(2)}) collective-permute-start(bf16[4,32,512]{2,1,0:T(8,128)(2,1)S(1)} %get-tuple-element.15), channel_id=1, source_target_pairs={{0,4},{4,0},{8,12},{12,8},{1,5},{5,1},{9,13},{13,9},{2,6},{6,2},{1... | collective-permute-start | bytes 393224 | tf_op jit(solution)/shard_map/ppermute | solution.py:160
  34.7 7.3 %collective-permute-start.16 = (bf16[4,32,512]{2,1,0:T(8,128)(2,1)S(1)}, bf16[4,32,512]{2,1,0:T(8,128)(2,1)S(1)}, u32[]{:S(2)}, u32[]{:S(2)}) collective-permute-start(bf16[4,32,512]{2,1,0:T(8,128)(2,1)S(1)} %get-tuple-element.16), channel_id=1, source_target_pairs={{0,8},{4,12},{8,0},{12,4},{1,9},{5,13},{9,1},{13,5},{2,10},{6,14},... | collective-permute-start | bytes 393224 | tf_op jit(solution)/shard_map/ppermute | solution.py:160
  36.2 7.4 %collective-permute-start.17 = (bf16[4,32,512]{2,1,0:T(8,128)(2,1)S(1)}, bf16[4,32,512]{2,1,0:T(8,128)(2,1)S(1)}, u32[]{:S(2)}, u32[]{:S(2)}) collective-permute-start(bf16[4,32,512]{2,1,0:T(8,128)(2,1)S(1)} %get-tuple-element.17), channel_id=1, source_target_pairs={{0,12},{4,8},{8,4},{12,0},{1,13},{5,9},{9,5},{13,1},{2,14},{6,10},... | collective-permute-start | bytes 393224 | tf_op jit(solution)/shard_map/ppermute | solution.py:160
  36.6 7.9 %collective-permute-start.9 = (bf16[4,32,512]{2,1,0:T(8,128)(2,1)S(1)}, bf16[4,32,512]{2,1,0:T(8,128)(2,1)S(1)}, u32[]{:S(2)}, u32[]{:S(2)}) collective-permute-start(bf16[4,32,512]{2,1,0:T(8,128)(2,1)S(1)} %get-tuple-element.11), channel_id=1, source_target_pairs={{0,4},{4,0},{8,12},{12,8},{1,5},{5,1},{9,13},{13,9},{2,6},{6,2},{1... | collective-permute-start | bytes 393224 | tf_op jit(solution)/shard_map/ppermute | solution.py:160
  38.2 9.1 %collective-permute-start.10 = (bf16[4,32,512]{2,1,0:T(8,128)(2,1)S(1)}, bf16[4,32,512]{2,1,0:T(8,128)(2,1)S(1)}, u32[]{:S(2)}, u32[]{:S(2)}) collective-permute-start(bf16[4,32,512]{2,1,0:T(8,128)(2,1)S(1)} %get-tuple-element.12), channel_id=1, source_target_pairs={{0,8},{4,12},{8,0},{12,4},{1,9},{5,13},{9,1},{13,5},{2,10},{6,14},... | collective-permute-start | bytes 393224 | tf_op jit(solution)/shard_map/ppermute | solution.py:160
  39.7 7.5 %collective-permute-start.11 = (bf16[4,32,512]{2,1,0:T(8,128)(2,1)S(1)}, bf16[4,32,512]{2,1,0:T(8,128)(2,1)S(1)}, u32[]{:S(2)}, u32[]{:S(2)}) collective-permute-start(bf16[4,32,512]{2,1,0:T(8,128)(2,1)S(1)} %get-tuple-element.13), channel_id=1, source_target_pairs={{0,12},{4,8},{8,4},{12,0},{1,13},{5,9},{9,5},{13,1},{2,14},{6,10},... | collective-permute-start | bytes 393224 | tf_op jit(solution)/shard_map/ppermute | solution.py:160
  43.7 16.4 %copy-start = (bf16[1024,512]{1,0:T(8,128)(2,1)S(1)}, bf16[1024,512]{1,0:T(8,128)(2,1)}, u32[]{:S(2)}) copy-start(bf16[1024,512]{1,0:T(8,128)(2,1)} %refs_2_.1) | copy-start | bytes 3145732
  43.7 5.4 %collective-permute-start.18 = (bf16[32,512]{1,0:T(8,128)(2,1)S(1)}, bf16[32,512]{1,0:T(8,128)(2,1)S(1)}, u32[]{:S(2)}, u32[]{:S(2)}) collective-permute-start(bf16[32,512]{1,0:T(8,128)(2,1)S(1)} %get-tuple-element.23), channel_id=1, source_target_pairs={{0,1},{1,0},{2,3},{3,2},{4,5},{5,4},{6,7},{7,6},{8,9},{9,8},{10,11... | collective-permute-start | bytes 98312 | tf_op jit(solution)/shard_map/ppermute | solution.py:160
  43.8 7.1 %collective-permute-start.20 = (bf16[32,512]{1,0:T(8,128)(2,1)S(1)}, bf16[32,512]{1,0:T(8,128)(2,1)S(1)}, u32[]{:S(2)}, u32[]{:S(2)}) collective-permute-start(bf16[32,512]{1,0:T(8,128)(2,1)S(1)} %get-tuple-element.24), channel_id=1, source_target_pairs={{0,3},{1,2},{2,1},{3,0},{4,7},{5,6},{6,5},{7,4},{8,11},{9,10},{10,... | collective-permute-start | bytes 98312 | tf_op jit(solution)/shard_map/ppermute | solution.py:160
  44.5 6.4 %collective-permute-start.19 = (bf16[32,512]{1,0:T(8,128)(2,1)S(1)}, bf16[32,512]{1,0:T(8,128)(2,1)S(1)}, u32[]{:S(2)}, u32[]{:S(2)}) collective-permute-start(bf16[32,512]{1,0:T(8,128)(2,1)S(1)} %get-tuple-element.25), channel_id=1, source_target_pairs={{0,2},{1,3},{2,0},{3,1},{4,6},{5,7},{6,4},{7,5},{8,10},{9,11},{10,... | collective-permute-start | bytes 98312 | tf_op jit(solution)/shard_map/ppermute | solution.py:160
  47.4 7.0 %collective-permute-start.12 = (bf16[32,512]{1,0:T(8,128)(2,1)S(1)}, bf16[32,512]{1,0:T(8,128)(2,1)S(1)}, u32[]{:S(2)}, u32[]{:S(2)}) collective-permute-start(bf16[32,512]{1,0:T(8,128)(2,1)S(1)} %get-tuple-element.20), channel_id=1, source_target_pairs={{0,1},{1,0},{2,3},{3,2},{4,5},{5,4},{6,7},{7,6},{8,9},{9,8},{10,11... | collective-permute-start | bytes 98312 | tf_op jit(solution)/shard_map/ppermute | solution.py:160
  48.4 7.0 %collective-permute-start.14 = (bf16[32,512]{1,0:T(8,128)(2,1)S(1)}, bf16[32,512]{1,0:T(8,128)(2,1)S(1)}, u32[]{:S(2)}, u32[]{:S(2)}) collective-permute-start(bf16[32,512]{1,0:T(8,128)(2,1)S(1)} %get-tuple-element.21), channel_id=1, source_target_pairs={{0,3},{1,2},{2,1},{3,0},{4,7},{5,6},{6,5},{7,4},{8,11},{9,10},{10,... | collective-permute-start | bytes 98312 | tf_op jit(solution)/shard_map/ppermute | solution.py:160
  49.1 6.3 %collective-permute-start.13 = (bf16[32,512]{1,0:T(8,128)(2,1)S(1)}, bf16[32,512]{1,0:T(8,128)(2,1)S(1)}, u32[]{:S(2)}, u32[]{:S(2)}) collective-permute-start(bf16[32,512]{1,0:T(8,128)(2,1)S(1)} %get-tuple-element.22), channel_id=1, source_target_pairs={{0,2},{1,3},{2,0},{3,1},{4,6},{5,7},{6,4},{7,5},{8,10},{9,11},{10,... | collective-permute-start | bytes 98312 | tf_op jit(solution)/shard_map/ppermute | solution.py:160
  51.0 5.8 %collective-permute-start.23 = (bf16[32,512]{1,0:T(8,128)(2,1)S(1)}, bf16[32,512]{1,0:T(8,128)(2,1)S(1)}, u32[]{:S(2)}, u32[]{:S(2)}) collective-permute-start(bf16[32,512]{1,0:T(8,128)(2,1)S(1)} %get-tuple-element.18), channel_id=1, source_target_pairs={{0,3},{1,2},{2,1},{3,0},{4,7},{5,6},{6,5},{7,4},{8,11},{9,10},{10,... | collective-permute-start | bytes 98312 | tf_op jit(solution)/shard_map/ppermute | solution.py:160
  53.3 4.8 %collective-permute-start.22 = (bf16[32,512]{1,0:T(8,128)(2,1)S(1)}, bf16[32,512]{1,0:T(8,128)(2,1)S(1)}, u32[]{:S(2)}, u32[]{:S(2)}) collective-permute-start(bf16[32,512]{1,0:T(8,128)(2,1)S(1)} %get-tuple-element.18), channel_id=1, source_target_pairs={{0,2},{1,3},{2,0},{3,1},{4,6},{5,7},{6,4},{7,5},{8,10},{9,11},{10,... | collective-permute-start | bytes 98312 | tf_op jit(solution)/shard_map/ppermute | solution.py:160
  54.4 4.1 %collective-permute-start.21 = (bf16[32,512]{1,0:T(8,128)(2,1)S(1)}, bf16[32,512]{1,0:T(8,128)(2,1)S(1)}, u32[]{:S(2)}, u32[]{:S(2)}) collective-permute-start(bf16[32,512]{1,0:T(8,128)(2,1)S(1)} %get-tuple-element.18), channel_id=1, source_target_pairs={{0,1},{1,0},{2,3},{3,2},{4,5},{5,4},{6,7},{7,6},{8,9},{9,8},{10,11... | collective-permute-start | bytes 98312 | tf_op jit(solution)/shard_map/ppermute | solution.py:160
  58.4 0.9 %copy-start.4 = (f32[1,2,32,512]{3,2,1,0:T(8,128)S(1)}, f32[1,2,32,512]{3,2,1,0:T(8,128)}, u32[]{:S(2)}) copy-start(f32[1,2,32,512]{3,2,1,0:T(8,128)} %param.6) | copy-start | bytes 393220
  58.5 1.8 %collective-permute-start.24 = (bf16[4,32,512]{2,1,0:T(8,128)(2,1)S(1)}, bf16[4,32,512]{2,1,0:T(8,128)(2,1)S(1)}, u32[]{:S(2)}, u32[]{:S(2)}) collective-permute-start(bf16[4,32,512]{2,1,0:T(8,128)(2,1)S(1)} %pad_maximum_fusion.1.refs_0_), channel_id=1, source_target_pairs={{0,16},{16,0},{1,17},{17,1},{2,18},{18,2},{3,19},{19,3},{4,20},{20... | collective-permute-start | bytes 393224 | tf_op jit(solution)/shard_map/ppermute | solution.py:160

commit v2 on v1

--- a/solution.py
+++ b/solution.py
@@ -222,12 +222,28 @@
     )
     imag_outs, real_outs = outs[:tile_count], outs[tile_count:]
 
-    imag_part, real_part = (
-        add_up(part[0], *[swap(part[k], "tile", k) for k in range(1, tile_count)]).astype(jnp.bfloat16)
-        for part in (imag_outs, real_outs)
-    )
-    imag_sum = add_up(imag_part[0], *[swap(imag_part[j], "cuts", j) for j in range(1, cuts_count)])[None]
-    own_real = add_up(real_part[0], *[swap(real_part[j], "cuts", j) for j in range(1, cuts_count)])
+    def spread_sum(terms, axis):
+        got = []
+        for step in range(1, len(terms)):
+            got.append(swap(terms[step], axis, step))
+        return add_up(terms[0], *got)
+
+    if angle_count > 1:
+        token = swap(imag_outs[0][0, :8, :LANES], "angle", 1)
+        anywhere = pl.BlockSpec(memory_space=pl.ANY)
+        going = pl.pallas_call(
+            lambda *refs: None,
+            out_shape=[jax.ShapeDtypeStruct(x.shape, x.dtype) for x in real_outs[1:]],
+            in_specs=[anywhere] * tile_count,
+            out_specs=[anywhere] * (tile_count - 1),
+            input_output_aliases={i: i for i in range(tile_count - 1)},
+            compiler_params=pltpu.CompilerParams(vmem_limit_bytes=2**20),
+        )(*real_outs[1:], token)
+        real_outs = [real_outs[0]] + list(going)
+    imag_part = spread_sum(imag_outs, "tile").astype(jnp.bfloat16)
+    real_part = spread_sum(list(real_outs), "tile").astype(jnp.bfloat16)
+    imag_sum = spread_sum(imag_part, "cuts")[None]
+    own_real = spread_sum(real_part, "cuts")
     share = jnp.stack([own_real, imag_sum[0]])
     new_objects = objects + share[None]
     phase = (object_half[1].astype(jnp.float32) + imag_sum).astype(jnp.bfloat16)

time: 61.4 us -> 61.3 us (level)
  starting transfers between devices: 34.6 us -> 32.6 us
  waiting for transfers between devices: 17.1 us -> 19 us
    ppermute x25 -> x26, starting transfers between devices: 34.6 us -> 32.6 us  [swap(): return lax.ppermute(x, axis, [(i, i ^ mask) for i in range(size)])]
    ppermute x25 -> x26, waiting for transfers between devices: 17.1 us -> 19 us  [swap(): return lax.ppermute(x, axis, [(i, i ^ mask) for i in range(size)])]
  transfers between devices with their start and end apart: 25 -> 26, of which waited for: 8 -> 10; matrix products, arithmetic and copies ran while one was open for 3% -> 3% of each run, Pallas kernels for 0% -> 0%
where the time goes in v2:
time: 61.3 us; the launch traced here: 61.1 us
  starting transfers between devices  32.6 us (53%)
  waiting for transfers between devices  19 us (31%)
  Pallas kernels  4.33 us (7%)
  other arithmetic  2.79 us (5%)
  local copies, waits for them, and re-layouts  1.6 us (3%)
  between operations  0.82 us (1%)
    ppermute x26, starting transfers between devices, swap(): return lax.ppermute(x, axis, [(i, i ^ mask) for i in range(size)])  32.6 us
    ppermute x26, waiting for transfers between devices, swap(): return lax.ppermute(x, axis, [(i, i ^ mask) for i in range(size)])  19 us
    pallas_call x1, Pallas kernels, compute(): pl.pallas_call(functools.partial(patch_kernel, layout), out_shape=[jax.Sh...  3.14 us
    convert_element_type x2, other arithmetic, compute(): object_half = objects[0].astype(jnp.bfloat16)  1.89 us
    unnamed x12, local copies, waits for them, and re-layouts  1.5 us
  transfers between devices with their start and end apart: 26, of which 10 were waited for; matrix products, arithmetic and copies ran while one was open for 3% of the time, Pallas kernels for 0%

profile of v2, /device:TPU:0, one launch (start us, length us, event | category | flops | bytes accessed | tf_op | source)
XLA Modules:
  0.0 61.1 jit_solution(11855325217469386342)
XLA Ops:
  0.6 1.0 %convert_bitcast_fusion = bf16[2,32,512]{2,1,0:T(8,128)(2,1)S(1)} fusion(f32[1,2,32,512]{3,2,1,0:T(8,128)} %param.6), kind=kLoop, calls=%fused_computation.26 | loop fusion | flops 32768 | bytes 196608 | tf_op jit(solution)/shard_map/convert_element_type | solution.py:178
  1.6 5.1 %collective-permute-start.2 = (bf16[2,32,512]{2,1,0:T(8,128)(2,1)S(1)}, bf16[2,32,512]{2,1,0:T(8,128)(2,1)S(1)}, u32[]{:S(2)}, u32[]{:S(2)}) collective-permute-start(bf16[2,32,512]{2,1,0:T(8,128)(2,1)S(1)} %convert_bitcast_fusion), channel_id=1, source_target_pairs={{0,3},{1,2},{2,1},{3,0},{4,7},{5,6},{6,5},{7,4},{8,11},{9,10},{10,... | collective-permute-start | bytes 196616 | tf_op jit(solution)/shard_map/ppermute | solution.py:160
  6.8 0.6 %collective-permute-start = (bf16[2,32,512]{2,1,0:T(8,128)(2,1)S(1)}, bf16[2,32,512]{2,1,0:T(8,128)(2,1)S(1)}, u32[]{:S(2)}, u32[]{:S(2)}) collective-permute-start(bf16[2,32,512]{2,1,0:T(8,128)(2,1)S(1)} %convert_bitcast_fusion), channel_id=1, source_target_pairs={{0,1},{1,0},{2,3},{3,2},{4,5},{5,4},{6,7},{7,6},{8,9},{9,8},{10,11... | collective-permute-start | bytes 196616 | tf_op jit(solution)/shard_map/ppermute | solution.py:160
  7.4 1.8 %collective-permute-done.2 = bf16[2,32,512]{2,1,0:T(8,128)(2,1)S(1)} collective-permute-done((bf16[2,32,512]{2,1,0:T(8,128)(2,1)S(1)}, bf16[2,32,512]{2,1,0:T(8,128)(2,1)S(1)}, u32[]{:S(2)}, u32[]{:S(2)}) %collective-permute-start.2) | collective-permute-done | bytes 65568 | tf_op jit(solution)/shard_map/ppermute | solution.py:160
  9.2 3.1 %collective-permute-done.1 = bf16[2,32,512]{2,1,0:T(8,128)(2,1)S(1)} collective-permute-done((bf16[2,32,512]{2,1,0:T(8,128)(2,1)S(1)}, bf16[2,32,512]{2,1,0:T(8,128)(2,1)S(1)}, u32[]{:S(2)}, u32[]{:S(2)}) %collective-permute-start.1) | collective-permute-done | bytes 65568 | tf_op jit(solution)/shard_map/ppermute | solution.py:160
  12.4 2.5 %collective-permute-start.8 = (bf16[3,2,32,512]{3,2,1,0:T(8,128)(2,1)S(1)}, bf16[3,2,32,512]{3,2,1,0:T(8,128)(2,1)S(1)}, u32[]{:S(2)}, u32[]{:S(2)}) collective-permute-start(bf16[3,2,32,512]{3,2,1,0:T(8,128)(2,1)S(1)} %pad_maximum_fusion.refs_1_), channel_id=1, source_target_pairs={{0,12},{4,8},{8,4},{12,0},{1,13},{5,9},{9,5},{13,1},{2,14},{6,10},... | collective-permute-start | bytes 589832 | tf_op jit(solution)/shard_map/ppermute | solution.py:160
  16.0 2.4 %collective-permute-start.5 = (bf16[2,32,512]{2,1,0:T(8,128)(2,1)S(1)}, bf16[2,32,512]{2,1,0:T(8,128)(2,1)S(1)}, u32[]{:S(2)}, u32[]{:S(2)}) collective-permute-start(bf16[2,32,512]{2,1,0:T(8,128)(2,1)S(1)} %convert_bitcast_fusion), channel_id=1, source_target_pairs={{0,12},{4,8},{8,4},{12,0},{1,13},{5,9},{9,5},{13,1},{2,14},{6,10},... | collective-permute-start | bytes 196616 | tf_op jit(solution)/shard_map/ppermute | solution.py:160
  18.9 6.6 %collective-permute-done.5 = bf16[2,32,512]{2,1,0:T(8,128)(2,1)S(1)} collective-permute-done((bf16[2,32,512]{2,1,0:T(8,128)(2,1)S(1)}, bf16[2,32,512]{2,1,0:T(8,128)(2,1)S(1)}, u32[]{:S(2)}, u32[]{:S(2)}) %collective-permute-start.5) | collective-permute-done | bytes 65568 | tf_op jit(solution)/shard_map/ppermute | solution.py:160
  25.6 1.6 %collective-permute-start.3 = (bf16[2,32,512]{2,1,0:T(8,128)(2,1)S(1)}, bf16[2,32,512]{2,1,0:T(8,128)(2,1)S(1)}, u32[]{:S(2)}, u32[]{:S(2)}) collective-permute-start(bf16[2,32,512]{2,1,0:T(8,128)(2,1)S(1)} %convert_bitcast_fusion), channel_id=1, source_target_pairs={{0,4},{4,0},{8,12},{12,8},{1,5},{5,1},{9,13},{13,9},{2,6},{6,2},{1... | collective-permute-start | bytes 196616 | tf_op jit(solution)/shard_map/ppermute | solution.py:160
  27.2 0.9 %convert_element_type.80.refs_0_ = bf16[1,2,32,512]{3,2,1,0:T(8,128)(2,1)S(1)} convert(f32[1,2,32,512]{3,2,1,0:T(8,128)} %param.6) | non-fusion elementwise | flops 32768 | bytes 196608 | tf_op jit(solution)/shard_map/convert_element_type | solution.py:178
  28.2 0.7 %copy-done.5 = s32[1,16,2]{1,2,0:T(2,128)S(1)} copy-done((s32[1,16,2]{1,2,0:T(2,128)S(1)}, s32[1,16,2]{1,2,0:T(2,128)}, u32[]{:S(2)}) %copy-start.5) | copy-done | bytes 152
  28.9 0.9 %collective-permute-done.3 = bf16[2,32,512]{2,1,0:T(8,128)(2,1)S(1)} collective-permute-done((bf16[2,32,512]{2,1,0:T(8,128)(2,1)S(1)}, bf16[2,32,512]{2,1,0:T(8,128)(2,1)S(1)}, u32[]{:S(2)}, u32[]{:S(2)}) %collective-permute-start.3) | collective-permute-done | bytes 65568 | tf_op jit(solution)/shard_map/ppermute | solution.py:160
  29.9 3.1 %shard_map.77 = (bf16[4,32,512]{2,1,0:T(8,128)(2,1)S(1)}, bf16[4,32,512]{2,1,0:T(8,128)(2,1)S(1)}, bf16[4,32,512]{2,1,0:T(8,128)(2,1)S(1)}, bf16[4,32,512]{2,1,0...) custom-call(s32[16,2]{1,0:T(8,128)S(1)} %copy.11.place_ref, ...), custom_call_target="tpu_custom_call" | custom-call | tf_op jit(solution)/shard_map/pallas_call | solution.py:198
  33.0 1.7 %collective-permute-start.16 = (bf16[4,32,512]{2,1,0:T(8,128)(2,1)S(1)}, bf16[4,32,512]{2,1,0:T(8,128)(2,1)S(1)}, u32[]{:S(2)}, u32[]{:S(2)}) collective-permute-start(bf16[4,32,512]{2,1,0:T(8,128)(2,1)S(1)} %get-tuple-element.21), channel_id=1, source_target_pairs={{0,4},{4,0},{8,12},{12,8},{1,5},{5,1},{9,13},{13,9},{2,6},{6,2},{1... | collective-permute-start | bytes 393224 | tf_op jit(solution)/shard_map/ppermute | solution.py:160
  34.7 1.5 %collective-permute-start.17 = (bf16[4,32,512]{2,1,0:T(8,128)(2,1)S(1)}, bf16[4,32,512]{2,1,0:T(8,128)(2,1)S(1)}, u32[]{:S(2)}, u32[]{:S(2)}) collective-permute-start(bf16[4,32,512]{2,1,0:T(8,128)(2,1)S(1)} %get-tuple-element.22), channel_id=1, source_target_pairs={{0,8},{4,12},{8,0},{12,4},{1,9},{5,13},{9,1},{13,5},{2,10},{6,14},... | collective-permute-start | bytes 393224 | tf_op jit(solution)/shard_map/ppermute | solution.py:160
  36.6 1.2 %collective-permute-done.9.refs_3_ = bf16[8,128]{1,0:T(8,128)(2,1)S(1)} collective-permute-done((bf16[8,128]{1,0:T(8,128)(2,1)S(1)}, bf16[8,128]{1,0:T(8,128)(2,1)S(1)}, u32[]{:S(2)}, u32[]{:S(2)}) %collective-permute-start.9) | collective-permute-done | bytes 2080 | tf_op jit(solution)/shard_map/ppermute | solution.py:160
  37.8 1.6 %collective-permute-start.10 = (bf16[4,32,512]{2,1,0:T(8,128)(2,1)S(1)}, bf16[4,32,512]{2,1,0:T(8,128)(2,1)S(1)}, u32[]{:S(2)}, u32[]{:S(2)}) collective-permute-start(bf16[4,32,512]{2,1,0:T(8,128)(2,1)S(1)} %get-tuple-element.18), channel_id=1, source_target_pairs={{0,4},{4,0},{8,12},{12,8},{1,5},{5,1},{9,13},{13,9},{2,6},{6,2},{1... | collective-permute-start | bytes 393224 | tf_op jit(solution)/shard_map/ppermute | solution.py:160
  39.4 1.5 %collective-permute-start.11 = (bf16[4,32,512]{2,1,0:T(8,128)(2,1)S(1)}, bf16[4,32,512]{2,1,0:T(8,128)(2,1)S(1)}, u32[]{:S(2)}, u32[]{:S(2)}) collective-permute-start(bf16[4,32,512]{2,1,0:T(8,128)(2,1)S(1)} %get-tuple-element.19), channel_id=1, source_target_pairs={{0,8},{4,12},{8,0},{12,4},{1,9},{5,13},{9,1},{13,5},{2,10},{6,14},... | collective-permute-start | bytes 393224 | tf_op jit(solution)/shard_map/ppermute | solution.py:160
  41.3 1.4 %collective-permute-done.18 = bf16[4,32,512]{2,1,0:T(8,128)(2,1)S(1)} collective-permute-done((bf16[4,32,512]{2,1,0:T(8,128)(2,1)S(1)}, bf16[4,32,512]{2,1,0:T(8,128)(2,1)S(1)}, u32[]{:S(2)}, u32[]{:S(2)}) %collective-permute-start.18) | collective-permute-done | bytes 131104 | tf_op jit(solution)/shard_map/ppermute | solution.py:160
  42.8 1.8 %collective-permute-start.21 = (bf16[32,512]{1,0:T(8,128)(2,1)S(1)}, bf16[32,512]{1,0:T(8,128)(2,1)S(1)}, u32[]{:S(2)}, u32[]{:S(2)}) collective-permute-start(bf16[32,512]{1,0:T(8,128)(2,1)S(1)} %get-tuple-element.30), channel_id=1, source_target_pairs={{0,3},{1,2},{2,1},{3,0},{4,7},{5,6},{6,5},{7,4},{8,11},{9,10},{10,... | collective-permute-start | bytes 98312 | tf_op jit(solution)/shard_map/ppermute | solution.py:160
  44.6 1.7 %collective-permute-start.20 = (bf16[32,512]{1,0:T(8,128)(2,1)S(1)}, bf16[32,512]{1,0:T(8,128)(2,1)S(1)}, u32[]{:S(2)}, u32[]{:S(2)}) collective-permute-start(bf16[32,512]{1,0:T(8,128)(2,1)S(1)} %get-tuple-element.31), channel_id=1, source_target_pairs={{0,2},{1,3},{2,0},{3,1},{4,6},{5,7},{6,4},{7,5},{8,10},{9,11},{10,... | collective-permute-start | bytes 98312 | tf_op jit(solution)/shard_map/ppermute | solution.py:160
  46.3 1.6 %collective-permute-done.11 = bf16[4,32,512]{2,1,0:T(8,128)(2,1)S(1)} collective-permute-done((bf16[4,32,512]{2,1,0:T(8,128)(2,1)S(1)}, bf16[4,32,512]{2,1,0:T(8,128)(2,1)S(1)}, u32[]{:S(2)}, u32[]{:S(2)}) %collective-permute-start.11) | collective-permute-done | bytes 131104 | tf_op jit(solution)/shard_map/ppermute | solution.py:160
  48.0 1.7 %collective-permute-start.15 = (bf16[32,512]{1,0:T(8,128)(2,1)S(1)}, bf16[32,512]{1,0:T(8,128)(2,1)S(1)}, u32[]{:S(2)}, u32[]{:S(2)}) collective-permute-start(bf16[32,512]{1,0:T(8,128)(2,1)S(1)} %get-tuple-element.27), channel_id=1, source_target_pairs={{0,3},{1,2},{2,1},{3,0},{4,7},{5,6},{6,5},{7,4},{8,11},{9,10},{10,... | collective-permute-start | bytes 98312 | tf_op jit(solution)/shard_map/ppermute | solution.py:160
  49.8 1.7 %collective-permute-start.14 = (bf16[32,512]{1,0:T(8,128)(2,1)S(1)}, bf16[32,512]{1,0:T(8,128)(2,1)S(1)}, u32[]{:S(2)}, u32[]{:S(2)}) collective-permute-start(bf16[32,512]{1,0:T(8,128)(2,1)S(1)} %get-tuple-element.28), channel_id=1, source_target_pairs={{0,2},{1,3},{2,0},{3,1},{4,6},{5,7},{6,4},{7,5},{8,10},{9,11},{10,... | collective-permute-start | bytes 98312 | tf_op jit(solution)/shard_map/ppermute | solution.py:160
  51.6 1.5 %collective-permute-start.24 = (bf16[32,512]{1,0:T(8,128)(2,1)S(1)}, bf16[32,512]{1,0:T(8,128)(2,1)S(1)}, u32[]{:S(2)}, u32[]{:S(2)}) collective-permute-start(bf16[32,512]{1,0:T(8,128)(2,1)S(1)} %get-tuple-element.24), channel_id=1, source_target_pairs={{0,3},{1,2},{2,1},{3,0},{4,7},{5,6},{6,5},{7,4},{8,11},{9,10},{10,... | collective-permute-start | bytes 98312 | tf_op jit(solution)/shard_map/ppermute | solution.py:160
  53.1 1.0 %collective-permute-start.23 = (bf16[32,512]{1,0:T(8,128)(2,1)S(1)}, bf16[32,512]{1,0:T(8,128)(2,1)S(1)}, u32[]{:S(2)}, u32[]{:S(2)}) collective-permute-start(bf16[32,512]{1,0:T(8,128)(2,1)S(1)} %get-tuple-element.24), channel_id=1, source_target_pairs={{0,2},{1,3},{2,0},{3,1},{4,6},{5,7},{6,4},{7,5},{8,10},{9,11},{10,... | collective-permute-start | bytes 98312 | tf_op jit(solution)/shard_map/ppermute | solution.py:160
  54.1 1.9 %collective-permute-start.22 = (bf16[32,512]{1,0:T(8,128)(2,1)S(1)}, bf16[32,512]{1,0:T(8,128)(2,1)S(1)}, u32[]{:S(2)}, u32[]{:S(2)}) collective-permute-start(bf16[32,512]{1,0:T(8,128)(2,1)S(1)} %get-tuple-element.24), channel_id=1, source_target_pairs={{0,1},{1,0},{2,3},{3,2},{4,5},{5,4},{6,7},{7,6},{8,9},{9,8},{10,11... | collective-permute-start | bytes 98312 | tf_op jit(solution)/shard_map/ppermute | solution.py:160
  56.1 1.3 %collective-permute-done.24 = bf16[32,512]{1,0:T(8,128)(2,1)S(1)} collective-permute-done((bf16[32,512]{1,0:T(8,128)(2,1)S(1)}, bf16[32,512]{1,0:T(8,128)(2,1)S(1)}, u32[]{:S(2)}, u32[]{:S(2)}) %collective-permute-start.24) | collective-permute-done | bytes 32800 | tf_op jit(solution)/shard_map/ppermute | solution.py:160
  57.3 0.8 %collective-permute-done.23 = bf16[32,512]{1,0:T(8,128)(2,1)S(1)} collective-permute-done((bf16[32,512]{1,0:T(8,128)(2,1)S(1)}, bf16[32,512]{1,0:T(8,128)(2,1)S(1)}, u32[]{:S(2)}, u32[]{:S(2)}) %collective-permute-start.23) | collective-permute-done | bytes 32800 | tf_op jit(solution)/shard_map/ppermute | solution.py:160
  58.4 0.8 %copy-done.4 = f32[1,2,32,512]{3,2,1,0:T(8,128)S(1)} copy-done((f32[1,2,32,512]{3,2,1,0:T(8,128)S(1)}, f32[1,2,32,512]{3,2,1,0:T(8,128)}, u32[]{:S(2)}) %copy-start.4) | copy-done | bytes 131096
  59.2 0.7 %fusion = f32[1,2,32,512]{3,2,1,0:T(8,128)} fusion(f32[1,2,32,512]{3,2,1,0:T(8,128)S(1)} %copy-done.4, f32[1,32,512]{2,1,0:T(8,128)S(1)} %get-tuple-element.25, f32[1,32,512]{2,1,0:T(8,128)S(1)} %fusion.6), kind=kLoop, calls=%fused_computation.4 | loop fusion | flops 65536 | bytes 393216 | tf_op jit(solution)/shard_map/add | solution.py:248
  60.2 1.0 %shard_map.80 = f32[128,512]{1,0:T(8,128)} custom-call(bf16[4,32,512]{2,1,0:T(8,128)(2,1)S(1)} %collective-permute-done.25.refs_0_, f32[128,512]{1,0:T(8,128)S(1)} %shard_map.79.refs_1_, bf16[1024,512]{1,0:T(8,128)(2,1)S(1)} %copy-done), custom_call_target="tpu_custom_call" | custom-call | tf_op jit(solution)/shard_map/pallas_call | solution.py:259
  (49 shorter events, 3.3 us)
Async XLA Ops:
  0.6 29.2 %copy-start.1 = (bf16[1,16,128,128]{3,2,1,0:T(8,128)(2,1)S(1)}, bf16[1,16,128,128]{3,2,1,0:T(8,128)(2,1)}, u32[]{:S(2)}) copy-start(bf16[1,16,128,128]{3,2,1,0:T(8,128)(2,1)} %param.9) | copy-start | bytes 1572868
  1.6 7.6 %collective-permute-start.2 = (bf16[2,32,512]{2,1,0:T(8,128)(2,1)S(1)}, bf16[2,32,512]{2,1,0:T(8,128)(2,1)S(1)}, u32[]{:S(2)}, u32[]{:S(2)}) collective-permute-start(bf16[2,32,512]{2,1,0:T(8,128)(2,1)S(1)} %convert_bitcast_fusion), channel_id=1, source_target_pairs={{0,3},{1,2},{2,1},{3,0},{4,7},{5,6},{6,5},{7,4},{8,11},{9,10},{10,... | collective-permute-start | bytes 196616 | tf_op jit(solution)/shard_map/ppermute | solution.py:160
  6.8 5.6 %collective-permute-start.1 = (bf16[2,32,512]{2,1,0:T(8,128)(2,1)S(1)}, bf16[2,32,512]{2,1,0:T(8,128)(2,1)S(1)}, u32[]{:S(2)}, u32[]{:S(2)}) collective-permute-start(bf16[2,32,512]{2,1,0:T(8,128)(2,1)S(1)} %convert_bitcast_fusion), channel_id=1, source_target_pairs={{0,2},{1,3},{2,0},{3,1},{4,6},{5,7},{6,4},{7,5},{8,10},{9,11},{10,... | collective-permute-start | bytes 196616 | tf_op jit(solution)/shard_map/ppermute | solution.py:160
  6.8 5.6 %collective-permute-start = (bf16[2,32,512]{2,1,0:T(8,128)(2,1)S(1)}, bf16[2,32,512]{2,1,0:T(8,128)(2,1)S(1)}, u32[]{:S(2)}, u32[]{:S(2)}) collective-permute-start(bf16[2,32,512]{2,1,0:T(8,128)(2,1)S(1)} %convert_bitcast_fusion), channel_id=1, source_target_pairs={{0,1},{1,0},{2,3},{3,2},{4,5},{5,4},{6,7},{7,6},{8,9},{9,8},{10,11... | collective-permute-start | bytes 196616 | tf_op jit(solution)/shard_map/ppermute | solution.py:160
  12.4 17.5 %copy-start.2 = (f32[2,128,128]{2,1,0:T(8,128)S(1)}, f32[2,128,128]{2,1,0:T(8,128)}, u32[]{:S(2)}) copy-start(f32[2,128,128]{2,1,0:T(8,128)} %refs_8_.1) | copy-start | bytes 393220
  12.4 17.5 %copy-start.3 = (bf16[2,128,128]{2,1,0:T(8,128)(2,1)S(1)}, bf16[2,128,128]{2,1,0:T(8,128)(2,1)}, u32[]{:S(2)}) copy-start(bf16[2,128,128]{2,1,0:T(8,128)(2,1)} %constant.2.clone.refs_10_) | copy-start | bytes 196612
  12.4 17.4 %collective-permute-start.8 = (bf16[3,2,32,512]{3,2,1,0:T(8,128)(2,1)S(1)}, bf16[3,2,32,512]{3,2,1,0:T(8,128)(2,1)S(1)}, u32[]{:S(2)}, u32[]{:S(2)}) collective-permute-start(bf16[3,2,32,512]{3,2,1,0:T(8,128)(2,1)S(1)} %pad_maximum_fusion.refs_1_), channel_id=1, source_target_pairs={{0,12},{4,8},{8,4},{12,0},{1,13},{5,9},{9,5},{13,1},{2,14},{6,10},... | collective-permute-start | bytes 589832 | tf_op jit(solution)/shard_map/ppermute | solution.py:160
  14.9 14.9 %collective-permute-start.7 = (bf16[3,2,32,512]{3,2,1,0:T(8,128)(2,1)S(1)}, bf16[3,2,32,512]{3,2,1,0:T(8,128)(2,1)S(1)}, u32[]{:S(2)}, u32[]{:S(2)}) collective-permute-start(bf16[3,2,32,512]{3,2,1,0:T(8,128)(2,1)S(1)} %pad_maximum_fusion.refs_1_), channel_id=1, source_target_pairs={{0,8},{4,12},{8,0},{12,4},{1,9},{5,13},{9,1},{13,5},{2,10},{6,14},... | collective-permute-start | bytes 589832 | tf_op jit(solution)/shard_map/ppermute | solution.py:160
  15.4 14.4 %collective-permute-start.6 = (bf16[3,2,32,512]{3,2,1,0:T(8,128)(2,1)S(1)}, bf16[3,2,32,512]{3,2,1,0:T(8,128)(2,1)S(1)}, u32[]{:S(2)}, u32[]{:S(2)}) collective-permute-start(bf16[3,2,32,512]{3,2,1,0:T(8,128)(2,1)S(1)} %pad_maximum_fusion.refs_1_), channel_id=1, source_target_pairs={{0,4},{4,0},{8,12},{12,8},{1,5},{5,1},{9,13},{13,9},{2,6},{6,2},{1... | collective-permute-start | bytes 589832 | tf_op jit(solution)/shard_map/ppermute | solution.py:160
  16.0 9.6 %collective-permute-start.5 = (bf16[2,32,512]{2,1,0:T(8,128)(2,1)S(1)}, bf16[2,32,512]{2,1,0:T(8,128)(2,1)S(1)}, u32[]{:S(2)}, u32[]{:S(2)}) collective-permute-start(bf16[2,32,512]{2,1,0:T(8,128)(2,1)S(1)} %convert_bitcast_fusion), channel_id=1, source_target_pairs={{0,12},{4,8},{8,4},{12,0},{1,13},{5,9},{9,5},{13,1},{2,14},{6,10},... | collective-permute-start | bytes 196616 | tf_op jit(solution)/shard_map/ppermute | solution.py:160
  18.4 10.5 %collective-permute-start.4 = (bf16[2,32,512]{2,1,0:T(8,128)(2,1)S(1)}, bf16[2,32,512]{2,1,0:T(8,128)(2,1)S(1)}, u32[]{:S(2)}, u32[]{:S(2)}) collective-permute-start(bf16[2,32,512]{2,1,0:T(8,128)(2,1)S(1)} %convert_bitcast_fusion), channel_id=1, source_target_pairs={{0,8},{4,12},{8,0},{12,4},{1,9},{5,13},{9,1},{13,5},{2,10},{6,14},... | collective-permute-start | bytes 196616 | tf_op jit(solution)/shard_map/ppermute | solution.py:160
  25.6 4.3 %collective-permute-start.3 = (bf16[2,32,512]{2,1,0:T(8,128)(2,1)S(1)}, bf16[2,32,512]{2,1,0:T(8,128)(2,1)S(1)}, u32[]{:S(2)}, u32[]{:S(2)}) collective-permute-start(bf16[2,32,512]{2,1,0:T(8,128)(2,1)S(1)} %convert_bitcast_fusion), channel_id=1, source_target_pairs={{0,4},{4,0},{8,12},{12,8},{1,5},{5,1},{9,13},{13,9},{2,6},{6,2},{1... | collective-permute-start | bytes 196616 | tf_op jit(solution)/shard_map/ppermute | solution.py:160
  28.1 0.7 %copy-start.5 = (s32[1,16,2]{1,2,0:T(2,128)S(1)}, s32[1,16,2]{1,2,0:T(2,128)}, u32[]{:S(2)}) copy-start(s32[1,16,2]{1,2,0:T(2,128)} %param.8) | copy-start | bytes 388
  33.0 7.9 %collective-permute-start.16 = (bf16[4,32,512]{2,1,0:T(8,128)(2,1)S(1)}, bf16[4,32,512]{2,1,0:T(8,128)(2,1)S(1)}, u32[]{:S(2)}, u32[]{:S(2)}) collective-permute-start(bf16[4,32,512]{2,1,0:T(8,128)(2,1)S(1)} %get-tuple-element.21), channel_id=1, source_target_pairs={{0,4},{4,0},{8,12},{12,8},{1,5},{5,1},{9,13},{13,9},{2,6},{6,2},{1... | collective-permute-start | bytes 393224 | tf_op jit(solution)/shard_map/ppermute | solution.py:160
  34.7 6.5 %collective-permute-start.17 = (bf16[4,32,512]{2,1,0:T(8,128)(2,1)S(1)}, bf16[4,32,512]{2,1,0:T(8,128)(2,1)S(1)}, u32[]{:S(2)}, u32[]{:S(2)}) collective-permute-start(bf16[4,32,512]{2,1,0:T(8,128)(2,1)S(1)} %get-tuple-element.22), channel_id=1, source_target_pairs={{0,8},{4,12},{8,0},{12,4},{1,9},{5,13},{9,1},{13,5},{2,10},{6,14},... | collective-permute-start | bytes 393224 | tf_op jit(solution)/shard_map/ppermute | solution.py:160
  36.2 6.4 %collective-permute-start.18 = (bf16[4,32,512]{2,1,0:T(8,128)(2,1)S(1)}, bf16[4,32,512]{2,1,0:T(8,128)(2,1)S(1)}, u32[]{:S(2)}, u32[]{:S(2)}) collective-permute-start(bf16[4,32,512]{2,1,0:T(8,128)(2,1)S(1)} %get-tuple-element.23), channel_id=1, source_target_pairs={{0,12},{4,8},{8,4},{12,0},{1,13},{5,9},{9,5},{13,1},{2,14},{6,10},... | collective-permute-start | bytes 393224 | tf_op jit(solution)/shard_map/ppermute | solution.py:160
  36.6 1.2 %collective-permute-start.9 = (bf16[8,128]{1,0:T(8,128)(2,1)S(1)}, bf16[8,128]{1,0:T(8,128)(2,1)S(1)}, u32[]{:S(2)}, u32[]{:S(2)}) collective-permute-start(bf16[8,128]{1,0:T(8,128)(2,1)S(1)} %slice_bitcast_fusion.9), channel_id=1, source_target_pairs={{0,16},{16,0},{1,17},{17,1},{2,18},{18,2},{3,19},{19,3},{4,20},{20... | collective-permute-start | bytes 6152 | tf_op jit(solution)/shard_map/ppermute | solution.py:160
  37.8 6.9 %collective-permute-start.10 = (bf16[4,32,512]{2,1,0:T(8,128)(2,1)S(1)}, bf16[4,32,512]{2,1,0:T(8,128)(2,1)S(1)}, u32[]{:S(2)}, u32[]{:S(2)}) collective-permute-start(bf16[4,32,512]{2,1,0:T(8,128)(2,1)S(1)} %get-tuple-element.18), channel_id=1, source_target_pairs={{0,4},{4,0},{8,12},{12,8},{1,5},{5,1},{9,13},{13,9},{2,6},{6,2},{1... | collective-permute-start | bytes 393224 | tf_op jit(solution)/shard_map/ppermute | solution.py:160
  39.4 8.5 %collective-permute-start.11 = (bf16[4,32,512]{2,1,0:T(8,128)(2,1)S(1)}, bf16[4,32,512]{2,1,0:T(8,128)(2,1)S(1)}, u32[]{:S(2)}, u32[]{:S(2)}) collective-permute-start(bf16[4,32,512]{2,1,0:T(8,128)(2,1)S(1)} %get-tuple-element.19), channel_id=1, source_target_pairs={{0,8},{4,12},{8,0},{12,4},{1,9},{5,13},{9,1},{13,5},{2,10},{6,14},... | collective-permute-start | bytes 393224 | tf_op jit(solution)/shard_map/ppermute | solution.py:160
  40.9 7.0 %collective-permute-start.12 = (bf16[4,32,512]{2,1,0:T(8,128)(2,1)S(1)}, bf16[4,32,512]{2,1,0:T(8,128)(2,1)S(1)}, u32[]{:S(2)}, u32[]{:S(2)}) collective-permute-start(bf16[4,32,512]{2,1,0:T(8,128)(2,1)S(1)} %get-tuple-element.20), channel_id=1, source_target_pairs={{0,12},{4,8},{8,4},{12,0},{1,13},{5,9},{9,5},{13,1},{2,14},{6,10},... | collective-permute-start | bytes 393224 | tf_op jit(solution)/shard_map/ppermute | solution.py:160
  42.7 17.2 %copy-start = (bf16[1024,512]{1,0:T(8,128)(2,1)S(1)}, bf16[1024,512]{1,0:T(8,128)(2,1)}, u32[]{:S(2)}) copy-start(bf16[1024,512]{1,0:T(8,128)(2,1)} %refs_2_.1) | copy-start | bytes 3145732
  42.8 7.0 %collective-permute-start.19 = (bf16[32,512]{1,0:T(8,128)(2,1)S(1)}, bf16[32,512]{1,0:T(8,128)(2,1)S(1)}, u32[]{:S(2)}, u32[]{:S(2)}) collective-permute-start(bf16[32,512]{1,0:T(8,128)(2,1)S(1)} %get-tuple-element.29), channel_id=1, source_target_pairs={{0,1},{1,0},{2,3},{3,2},{4,5},{5,4},{6,7},{7,6},{8,9},{9,8},{10,11... | collective-permute-start | bytes 98312 | tf_op jit(solution)/shard_map/ppermute | solution.py:160
  42.8 8.7 %collective-permute-start.21 = (bf16[32,512]{1,0:T(8,128)(2,1)S(1)}, bf16[32,512]{1,0:T(8,128)(2,1)S(1)}, u32[]{:S(2)}, u32[]{:S(2)}) collective-permute-start(bf16[32,512]{1,0:T(8,128)(2,1)S(1)} %get-tuple-element.30), channel_id=1, source_target_pairs={{0,3},{1,2},{2,1},{3,0},{4,7},{5,6},{6,5},{7,4},{8,11},{9,10},{10,... | collective-permute-start | bytes 98312 | tf_op jit(solution)/shard_map/ppermute | solution.py:160
  44.6 6.9 %collective-permute-start.20 = (bf16[32,512]{1,0:T(8,128)(2,1)S(1)}, bf16[32,512]{1,0:T(8,128)(2,1)S(1)}, u32[]{:S(2)}, u32[]{:S(2)}) collective-permute-start(bf16[32,512]{1,0:T(8,128)(2,1)S(1)} %get-tuple-element.31), channel_id=1, source_target_pairs={{0,2},{1,3},{2,0},{3,1},{4,6},{5,7},{6,4},{7,5},{8,10},{9,11},{10,... | collective-permute-start | bytes 98312 | tf_op jit(solution)/shard_map/ppermute | solution.py:160
  48.0 6.1 %collective-permute-start.13 = (bf16[32,512]{1,0:T(8,128)(2,1)S(1)}, bf16[32,512]{1,0:T(8,128)(2,1)S(1)}, u32[]{:S(2)}, u32[]{:S(2)}) collective-permute-start(bf16[32,512]{1,0:T(8,128)(2,1)S(1)} %get-tuple-element.26), channel_id=1, source_target_pairs={{0,1},{1,0},{2,3},{3,2},{4,5},{5,4},{6,7},{7,6},{8,9},{9,8},{10,11... | collective-permute-start | bytes 98312 | tf_op jit(solution)/shard_map/ppermute | solution.py:160
  48.0 8.0 %collective-permute-start.15 = (bf16[32,512]{1,0:T(8,128)(2,1)S(1)}, bf16[32,512]{1,0:T(8,128)(2,1)S(1)}, u32[]{:S(2)}, u32[]{:S(2)}) collective-permute-start(bf16[32,512]{1,0:T(8,128)(2,1)S(1)} %get-tuple-element.27), channel_id=1, source_target_pairs={{0,3},{1,2},{2,1},{3,0},{4,7},{5,6},{6,5},{7,4},{8,11},{9,10},{10,... | collective-permute-start | bytes 98312 | tf_op jit(solution)/shard_map/ppermute | solution.py:160
  49.8 6.2 %collective-permute-start.14 = (bf16[32,512]{1,0:T(8,128)(2,1)S(1)}, bf16[32,512]{1,0:T(8,128)(2,1)S(1)}, u32[]{:S(2)}, u32[]{:S(2)}) collective-permute-start(bf16[32,512]{1,0:T(8,128)(2,1)S(1)} %get-tuple-element.28), channel_id=1, source_target_pairs={{0,2},{1,3},{2,0},{3,1},{4,6},{5,7},{6,4},{7,5},{8,10},{9,11},{10,... | collective-permute-start | bytes 98312 | tf_op jit(solution)/shard_map/ppermute | solution.py:160
  51.6 5.8 %collective-permute-start.24 = (bf16[32,512]{1,0:T(8,128)(2,1)S(1)}, bf16[32,512]{1,0:T(8,128)(2,1)S(1)}, u32[]{:S(2)}, u32[]{:S(2)}) collective-permute-start(bf16[32,512]{1,0:T(8,128)(2,1)S(1)} %get-tuple-element.24), channel_id=1, source_target_pairs={{0,3},{1,2},{2,1},{3,0},{4,7},{5,6},{6,5},{7,4},{8,11},{9,10},{10,... | collective-permute-start | bytes 98312 | tf_op jit(solution)/shard_map/ppermute | solution.py:160
  53.1 5.1 %collective-permute-start.23 = (bf16[32,512]{1,0:T(8,128)(2,1)S(1)}, bf16[32,512]{1,0:T(8,128)(2,1)S(1)}, u32[]{:S(2)}, u32[]{:S(2)}) collective-permute-start(bf16[32,512]{1,0:T(8,128)(2,1)S(1)} %get-tuple-element.24), channel_id=1, source_target_pairs={{0,2},{1,3},{2,0},{3,1},{4,6},{5,7},{6,4},{7,5},{8,10},{9,11},{10,... | collective-permute-start | bytes 98312 | tf_op jit(solution)/shard_map/ppermute | solution.py:160
  54.1 4.3 %collective-permute-start.22 = (bf16[32,512]{1,0:T(8,128)(2,1)S(1)}, bf16[32,512]{1,0:T(8,128)(2,1)S(1)}, u32[]{:S(2)}, u32[]{:S(2)}) collective-permute-start(bf16[32,512]{1,0:T(8,128)(2,1)S(1)} %get-tuple-element.24), channel_id=1, source_target_pairs={{0,1},{1,0},{2,3},{3,2},{4,5},{5,4},{6,7},{7,6},{8,9},{9,8},{10,11... | collective-permute-start | bytes 98312 | tf_op jit(solution)/shard_map/ppermute | solution.py:160
  58.3 0.9 %copy-start.4 = (f32[1,2,32,512]{3,2,1,0:T(8,128)S(1)}, f32[1,2,32,512]{3,2,1,0:T(8,128)}, u32[]{:S(2)}) copy-start(f32[1,2,32,512]{3,2,1,0:T(8,128)} %param.6) | copy-start | bytes 393220
  58.4 1.8 %collective-permute-start.25 = (bf16[4,32,512]{2,1,0:T(8,128)(2,1)S(1)}, bf16[4,32,512]{2,1,0:T(8,128)(2,1)S(1)}, u32[]{:S(2)}, u32[]{:S(2)}) collective-permute-start(bf16[4,32,512]{2,1,0:T(8,128)(2,1)S(1)} %pad_maximum_fusion.1.refs_0_), channel_id=1, source_target_pairs={{0,16},{16,0},{1,17},{17,1},{2,18},{18,2},{3,19},{19,3},{4,20},{20... | collective-permute-start | bytes 393224 | tf_op jit(solution)/shard_map/ppermute | solution.py:160
